TPU v7x, 32 devices: a whole 2x2x4 slice. The times are simulated.
32 devices in a mesh: groups: 2 (over y), cell: 4 (over z), sc: 4 (over x, core).
Axes of the slice: x: 2, y: 2, z: 4, core: 2. Of those that a mesh axis runs over, the one named last changes fastest.
Arguments:
- symbols: bfloat16 [32, 2, 32, 4096], P(('groups', 'cell'), None, None, 'sc'), parts along dimension 0, may hold values from -4 to 4
- precoders: bfloat16 [32, 64, 16, 128], P(('groups', 'cell'), 'sc'), parts along dimension 0, may hold values from -1 to 1
- plan: int32 [32], P(('groups', 'cell')), parts along dimension 0, may hold values 0 or 1
- own_channel: bfloat16 [32, 16, 64, 128], P(('groups', 'cell'), None, 'sc'), parts along dimension 0, may hold values from -0.5 to 0.5
- cross_channel: bfloat16 [32, 16, 4, 64, 128], P(('groups', 'cell'), None, None, 'sc'), parts along dimension 0, may hold values from -0.375 to 0.375
- neighbours: int32 [32, 4], P(('groups', 'cell')), parts along dimension 0, may hold values from 0 to 15, as said below
- noise: bfloat16 [32, 16, 2, 2, 4096], P(('groups', 'cell'), None, None, None, 'sc'), parts along dimension 0, may hold values from -2 to 2
Outputs:
- time_signal: bfloat16 [32, 16, 2, 2, 4096], P(('groups', 'cell'), 'sc'), parts along dimension 0
There are 2 independent parts, one for each index of `groups`. A program takes and returns all parts, laid end to end along the dimension named above; each array names one. Nothing has to cross between parts.
Inputs may be any that keep to these rules, and one draw needn't show every extreme that they name: `neighbours`: each cell's 4 entries are distinct cells other than itself, each within 4 cells of it along the cycle of all 16 cells, where cell 0 follows cell 16 - 1.
All inputs are finite; a program needn't handle non-finite values. No bound on the sum of `plan` on one device may be relied on, other than what follows from the above.
Results may differ from a plain program's by a relative error of at most 0.0057.
Values may be sent and summed in bfloat16 or wider, within the bound.
No kernel may reach another device: no remote copies, remote signals or barrier semaphores. Data moves between devices by JAX's collectives and lax.ppermute only.
A program may use at most 64 MiB of HBM per device.

v0:
```python
import functools
import math

import jax
import jax.numpy as jnp
import numpy as np
from jax import lax
from jax.experimental import pallas as pl
from jax.experimental.pallas import tpu as pltpu
from jax.sharding import PartitionSpec as P


LANES = 128
SMEM = pltpu.MemorySpace.SMEM
BF16, F32 = jnp.bfloat16, jnp.float32
NT = (((1,), (1,)), ((), ()))


def partner(me, d, parts):
    return (me + d) % parts


def gate_kernel(chunks, plan_ref, x_ref, *outs):
    cells, _, streams, _ = x_ref.shape
    for c in range(cells):
        on = plan_ref[c] != 0
        for out, (t, first, count) in zip(outs, chunks):
            x = x_ref[c, t, :, first * LANES : (first + count) * LANES]
            out[c * streams : (c + 1) * streams] = jnp.where(on, x, jnp.zeros_like(x))


def place(near_ref, base_ref, total, cells, slots):
    table = []
    for c in range(cells):
        row = []
        for k in range(slots):
            at = near_ref[c, k] - base_ref[0] + cells
            at = jnp.where(at < 0, at + total, at)
            row.append(jnp.where(at >= total, at - total, at))
        table.append(row)
    return table


def combined_channel(masks, h, p):
    cells = p.shape[0]
    slots = len(masks[0])
    users = h.shape[0] // (slots * cells)
    half = p.shape[-1] // 2
    wide = p.astype(F32)
    lane = lax.broadcasted_iota(jnp.int32, wide.shape[1:], 1)
    p0 = [jnp.where(lane < half, wide[n], -wide[n]) for n in range(cells)]
    p1 = [pltpu.roll(wide[n], half, 1) for n in range(cells)]
    rows = [r for n in range(cells) for r in (p0[n], -p1[n])] + [r for n in range(cells) for r in (p1[n], p0[n])]
    rhs = jnp.concatenate(rows, axis=0).astype(BF16)
    prod = lax.dot_general(h, rhs, NT, preferred_element_type=F32)
    width = prod.shape[1] // 2
    out = []
    for z in range(2):
        for c in range(cells):
            acc = jnp.zeros((users, width), F32)
            for k in range(slots):
                start = (k * cells + c) * users
                part = prod[start : start + users, z * width : (z + 1) * width]
                acc = jnp.where(masks[c][k], part, acc)
            out.append(acc)
    return jnp.concatenate(out, axis=0).astype(BF16)


def source_masks(table, base, users, cells, width):
    source = lax.broadcasted_iota(jnp.int32, (users, width), 1) // (width // cells) + base
    return [[source == at for at in row] for row in table]


def pick_subbands(res, per):
    rows = res.shape[0] // per
    lane = lax.broadcasted_iota(jnp.int32, (rows, LANES), 1) // (LANES // per)
    out = res[:rows]
    for i in range(1, per):
        out = jnp.where(lane == i, res[i * rows : (i + 1) * rows], out)
    return out


def own_kernel(total, chunks, near_ref, base_ref, h_ref, own_ref, p_ref, *refs):
    s_refs, acc_refs = refs[: len(chunks)], refs[len(chunks) :]
    blocks = max(first + count for _, first, count in chunks)
    subbands, cells = p_ref.shape[1], p_ref.shape[0]
    per = subbands // blocks
    users = own_ref.shape[1] // cells
    table = place(near_ref, base_ref, total, cells, h_ref.shape[1] // (cells * users))
    table = [row + [cells + c] for c, row in enumerate(table)]
    masks = source_masks(table, cells, users, cells, s_refs[0].shape[0])
    for r in range(blocks):
        g = []
        for b in range(r * per, (r + 1) * per):
            h = jnp.concatenate([h_ref[b], own_ref[b]], axis=0)
            g.append(combined_channel(masks, h, p_ref[:, b]))
        g = jnp.concatenate(g, axis=0)
        for s_ref, acc_ref, (_, first, count) in zip(s_refs, acc_refs, chunks):
            if first <= r < first + count:
                at = r - first
                res = jnp.dot(g, s_ref[:, at * LANES : (at + 1) * LANES], preferred_element_type=F32)
                acc_ref[at] = pick_subbands(res, per)


def remote_kernel(total, users, near_ref, base_ref, h_ref, a_ref, b_ref, g_ref):
    subbands, cells = a_ref.shape[1], a_ref.shape[0]
    blocks = g_ref.shape[0]
    per = subbands // blocks
    width = g_ref.shape[2] // 2
    rows = 2 * cells * users
    table = place(near_ref, base_ref, total, cells, h_ref.shape[1] // (cells * users))
    for side, (ref, base) in enumerate(((a_ref, 0), (b_ref, 2 * cells))):
        masks = source_masks(table, base, users, cells, width)
        for b in range(subbands):
            r, i = divmod(b, per)
            g_ref[r, i * rows : (i + 1) * rows, side * width : (side + 1) * width] = combined_channel(
                masks, h_ref[b], ref[:, b]
            )


def grid_kernel(chunk, me_ref, g_ref, a_ref, b_ref, acc_ref, noise_ref, *refs):
    outs, y, turned, tiles = refs[:-3], refs[-3], refs[-2], refs[-1]
    t, start, _ = chunk
    blocks, rows, _ = acc_ref.shape
    per = g_ref.shape[1] // rows
    _, users = noise_ref.shape[:2]
    for r in range(blocks):
        lanes = slice(r * LANES, (r + 1) * LANES)
        s = jnp.concatenate([a_ref[:, lanes], b_ref[:, lanes]], axis=0)
        res = jnp.dot(g_ref[start + r], s, preferred_element_type=F32)
        y[r * rows : (r + 1) * rows] = acc_ref[r] + pick_subbands(res, per)
    half = rows // 2
    step = 8
    for first in range(0, half, step):
        for part in range(2 * blocks // step):
            src = [divmod(part * step + i, 2) for i in range(step)]
            group = [y[r * rows + z * half + first : r * rows + z * half + first + step] for r, z in src]
            turned[part, first : first + step] = jnp.swapaxes(jnp.stack(group), 0, 1)
    for row in range(half):
        c, u = divmod(row, users)
        tile = jnp.concatenate([turned[part, row] for part in range(2 * blocks // step)], axis=0)
        tiles[u, c] = (tile + noise_ref[c, u, t, 2 * start : 2 * (start + blocks)].astype(F32)).astype(BF16)
    count = len(outs)
    for d in range(count):
        group = partner(me_ref[0], d, count)
        outs[d][...] = tiles[pl.ds(group * (users // count), users // count)]


def swap_groups(parts, width):
    parts = list(parts)
    lane = lax.broadcasted_iota(jnp.int32, parts[0].shape, 1)
    step = len(parts) // 2
    while step:
        low = (lane // (width * step)) % 2 == 0
        for i in range(len(parts)):
            if i & step == 0:
                x, y = parts[i], parts[i + step]
                parts[i] = jnp.where(low, x, pltpu.roll(y, width * step, 1))
                parts[i + step] = jnp.where(low, pltpu.roll(x, LANES - width * step, 1), y)
        step //= 2
    return parts


def time_kernel(t, halves, w1_ref, tw_ref, w2_ref, *refs):
    out_ref, held, sems = refs[-3:]
    rows = tw_ref.shape[1]
    share, cells, tall, _ = refs[0].shape
    parts = refs[: 2 * rows // tall]
    seqs = share * cells
    per = LANES // rows
    w1 = w1_ref[...]
    w2 = w2_ref[...]
    n2 = w2.shape[0] // 2
    tall = n2 // per
    batch = min(seqs, 2 * per)
    held_as = BF16 if halves == 1 else F32
    copies = []
    for first in range(0, seqs, batch):
        data = [
            jnp.concatenate([p[q // cells, q % cells].astype(held_as) for p in parts], axis=0)
            for q in range(first, first + batch)
        ]
        data = jnp.concatenate(data, axis=1).astype(BF16)
        both = jnp.dot(w1, data, preferred_element_type=F32)
        both = both[: 2 * rows] + both[2 * rows :]
        turned = []
        for q in range(batch):
            re = both[:rows, q * LANES : (q + 1) * LANES]
            im = both[rows:, q * LANES : (q + 1) * LANES]
            turned.append(
                jnp.concatenate([re * tw_ref[0] - im * tw_ref[1], re * tw_ref[1] + im * tw_ref[0]], axis=1)
            )
        turned = jnp.concatenate(turned, axis=0)
        high = turned.astype(BF16)
        low = (turned - high.astype(F32)).astype(BF16)
        prod = lax.dot_general(w2, high, NT, preferred_element_type=F32)
        prod = prod[:n2] + prod[n2:] + lax.dot_general(w2[:n2], low, NT, preferred_element_type=F32)
        for quad in range(batch // per):
            lanes = slice(quad * LANES, (quad + 1) * LANES)
            pieces = swap_groups([prod[i * tall : (i + 1) * tall, lanes].astype(BF16) for i in range(per)], rows)
            for at, piece in enumerate(pieces):
                u, c = divmod(first + quad * per + at, cells)
                held[u, c] = piece
                if c == cells - 1:
                    copies.append(pltpu.make_async_copy(held.at[u], out_ref.at[:, u, t], sems.at[u]))
                    copies[-1].start()
    for copy in copies:
        copy.wait()


def rotation(angle):
    return np.block([[np.cos(angle), -np.sin(angle)], [np.sin(angle), np.cos(angle)]])


def split_rows(table):
    high = table.astype(jnp.bfloat16)
    low = (table - high.astype(np.float64)).astype(jnp.bfloat16)
    return np.concatenate([high, low], axis=0)


def tables(length, parts):
    rows = length // LANES
    local = rows // parts
    m = np.arange(rows)
    w1 = []
    for me in range(parts):
        source = [(me - d) % parts for d in range(parts)]
        order = np.concatenate([src * local + np.arange(local) for src in source])
        angle = 2 * np.pi * (np.outer(m, order) % rows) / rows
        full = rotation(angle).reshape(2 * rows, 2, rows).transpose(0, 2, 1).reshape(2 * rows, 2 * rows)
        w1.append(split_rows(full))
    lane = np.arange(LANES)
    angle = 2 * np.pi * (np.outer(m, lane) % length) / length
    twist = (np.stack([np.cos(angle), np.sin(angle)]) / math.sqrt(length)).astype(np.float32)
    per = LANES // rows
    angle = 2 * np.pi * (np.outer(lane, lane) % LANES) / LANES
    w2 = rotation(angle).reshape(2, rows, per, 2 * LANES).transpose(2, 1, 0, 3).reshape(2 * LANES, 2 * LANES)
    return np.stack(w1), twist, split_rows(w2)


def body(symbols, precoders, plan, own_channel, cross_channel, neighbours, noise):
    cells, times, streams, width = symbols.shape
    subbands, users, slots, ants = precoders.shape[1], own_channel.shape[1], cross_channel.shape[2], precoders.shape[3]
    blocks = width // LANES
    per = subbands // blocks
    parts = lax.axis_size("sc")
    ring = lax.axis_size("cell")
    length = width * parts
    rows = 2 * cells * users
    up = [(i, (i + 1) % ring) for i in range(ring)]
    down = [(j, i) for i, j in up]

    def both_ways(x):
        moved = []
        for pairs in (up, down):
            moved.append(lax.ppermute(x, "cell", pairs))
        return moved

    total = cells * ring
    tall = cells * streams
    vmem = pl.BlockSpec(memory_space=pltpu.MemorySpace.VMEM)
    smem = pl.BlockSpec(memory_space=SMEM)
    hbm = pl.BlockSpec(memory_space=pltpu.MemorySpace.HBM)

    def call(kernel, out_shape, ins, scalars, scratch=(), grant=16, flops=1_000_000_000, **more):
        return pl.pallas_call(
            kernel,
            in_specs=[smem] * scalars + [vmem] * (len(ins) - scalars),
            out_specs=jax.tree.map(lambda _: vmem, out_shape),
            out_shape=out_shape,
            scratch_shapes=scratch,
            compiler_params=pltpu.CompilerParams(vmem_limit_bytes=grant << 20),
            cost_estimate=pl.CostEstimate(flops=flops, bytes_accessed=4_000_000, transcendentals=0),
        )(*ins)

    p_before, p_after = both_ways(precoders)
    chunks = [(t, 0, blocks) for t in range(times - 1)]
    cut = blocks // 2
    chunks += [(times - 1, 0, cut), (times - 1, cut, blocks - cut)]
    gated = call(
        functools.partial(gate_kernel, chunks),
        [jax.ShapeDtypeStruct((tall, count * LANES), BF16) for _, _, count in chunks], (plan, symbols), 1,
    )
    halos = [both_ways(g) for g in gated]

    base = (lax.axis_index("cell") * cells).astype(jnp.int32)[None]
    me = lax.axis_index("sc").astype(jnp.int32)[None]
    cross = cross_channel.transpose(3, 2, 0, 1, 4).reshape(subbands, slots * cells * users, ants)
    own = own_channel.transpose(2, 0, 1, 3).reshape(subbands, cells * users, ants)
    noise_tiles = noise.reshape(cells, users, times, 2, blocks, LANES).transpose(0, 1, 2, 4, 3, 5)
    noise_tiles = noise_tiles.reshape(cells, users, times, 2 * blocks, LANES)

    acc = call(
        functools.partial(own_kernel, total, chunks),
        [jax.ShapeDtypeStruct((count, rows, LANES), F32) for _, _, count in chunks],
        (neighbours, base, cross, own, precoders, *gated), 2,
    )
    comb = call(
        functools.partial(remote_kernel, total, users),
        jax.ShapeDtypeStruct((blocks, per * rows, 2 * tall), BF16),
        (neighbours, base, cross, p_before, p_after), 2,
    )

    w1, twist, w2 = (jnp.asarray(x) for x in tables(length, parts))
    w1 = lax.dynamic_index_in_dim(w1, me[0], 0, False)
    share = users // parts
    full = (cells, share, times, 2 * length // LANES, LANES)
    out, got = None, []
    for at, (chunk, halo) in enumerate(zip(chunks, halos)):
        t, _, count = chunk
        tile = (share, cells, 2 * count, LANES)
        sent = call(
            functools.partial(grid_kernel, chunk), [jax.ShapeDtypeStruct(tile, BF16)] * parts,
            (me, comb, *halo, acc[at], noise_tiles), 1,
            scratch=[
                pltpu.VMEM((count * rows, LANES), F32),
                pltpu.VMEM((2 * count // 8, rows // 2, 8, LANES), F32),
                pltpu.VMEM((users, cells, 2 * count, LANES), BF16),
            ],
        )
        moved = {d: lax.ppermute(sent[d], "sc", [(i, (i ^ d) if ([0, 0, 0])[at] else (i + d) % parts) for i in range(parts)]) for d in ([(3,2,1),(3,2,1),(2,1,3)])[at]}
        got.append([sent[0]] + [moved[d] for d in range(1, parts)])
        if at + 1 < len(chunks) and chunks[at + 1][0] == t:
            continue
        halves = len(got)
        arrived = [got[h][d] for d in range(parts) for h in range(halves)]
        got = []
        ins = (w1, twist, w2, *arrived) + (() if out is None else (out,))
        out = pl.pallas_call(
            functools.partial(time_kernel, t, halves),
            in_specs=[vmem] * (3 + len(arrived)) + [hbm] * (t > 0),
            out_specs=hbm,
            out_shape=jax.ShapeDtypeStruct(full, BF16),
            input_output_aliases={3 + len(arrived): 0} if t else {},
            scratch_shapes=[
                pltpu.VMEM((share, cells, 2 * length // LANES, LANES), BF16),
                pltpu.SemaphoreType.DMA((share,)),
            ],
            name="time",
            compiler_params=pltpu.CompilerParams(vmem_limit_bytes=16 << 20),
            cost_estimate=pl.CostEstimate(flops=1_000_000_000, bytes_accessed=2_000_000, transcendentals=0),
        )(*ins)
    out = out.reshape(cells, share, times, length // LANES, 2, LANES).transpose(0, 1, 2, 4, 3, 5)
    return out.reshape(cells, share, times, 2, length)


def solution(mesh):
    in_specs = (
        P(("groups", "cell"), None, None, "sc"),
        P(("groups", "cell"), "sc", None, None),
        P(("groups", "cell")),
        P(("groups", "cell"), None, "sc", None),
        P(("groups", "cell"), None, None, "sc", None),
        P(("groups", "cell"), None),
        P(("groups", "cell"), None, None, None, "sc"),
    )
    out_specs = P(("groups", "cell"), "sc", None, None, None)
    return jax.shard_map(body, mesh=mesh, in_specs=in_specs, out_specs=out_specs, check_vma=False)
```

profile of v0, /device:TPU:1, one launch (start us, length us, event | category | flops | bytes accessed | tf_op | source)
XLA Modules:
  0.0 47.4 jit_solution(14116630816312260193)
XLA Ops:
  0.0 2.1 %collective-permute-start = (bf16[4,16,16,128]{3,2,1,0:T(8,128)(2,1)}, bf16[4,16,16,128]{3,2,1,0:T(8,128)(2,1)S(1)}, u32[]{:S(2)}, u32[]{:S(2)}) collective-permute-start(bf16[4,16,16,128]{3,2,1,0:T(8,128)(2,1)} %p_ref.1), channel_id=1, source_target_pairs={{0,4},{4,8},{8,12},{12,0},{1,5},{5,9},{9,13},{13,1},{2,6},{6,10},{... | collective-permute-start | bytes 786440 | tf_op jit(solution)/shard_map/ppermute | solution.py:256
  2.1 2.0 %collective-permute-start.1 = (bf16[4,16,16,128]{3,2,1,0:T(8,128)(2,1)}, bf16[4,16,16,128]{3,2,1,0:T(8,128)(2,1)S(1)}, u32[]{:S(2)}, u32[]{:S(2)}) collective-permute-start(bf16[4,16,16,128]{3,2,1,0:T(8,128)(2,1)} %p_ref.1), channel_id=1, source_target_pairs={{4,0},{8,4},{12,8},{0,12},{5,1},{9,5},{13,9},{1,13},{6,2},{10,6},{... | collective-permute-start | bytes 786440 | tf_op jit(solution)/shard_map/ppermute | solution.py:256
  4.1 1.0 %copy-done = bf16[4,2,32,1024]{3,2,1,0:T(8,128)(2,1)S(1)} copy-done((bf16[4,2,32,1024]{3,2,1,0:T(8,128)(2,1)S(1)}, bf16[4,2,32,1024]{3,2,1,0:T(8,128)(2,1)}, u32[]{:S(2)}) %copy-start) | copy-done | bytes 524312
  5.2 0.7 %copy-done.4 = s32[4]{0:T(128)S(1)} copy-done((s32[4]{0:T(128)S(1)}, s32[4]{0:T(128)}, u32[]{:S(2)}) %copy-start.4) | copy-done | bytes 40
  5.8 0.6 %shard_map.101 = (bf16[128,1024]{1,0:T(8,128)(2,1)S(1)}, bf16[128,512]{1,0:T(8,128)(2,1)S(1)}, bf16[128,512]{1,0:T(8,128)(2,1)S(1)}) custom-call(s32[4]{0:T(128)S(1)} %copy-done.4, bf16[4,2,32,1024]{3,2,1,0:T(8,128)(2,1)S(1)} %copy-done), custom_call_target="tpu_custom_call" | custom-call | flops 1000000000 | bytes 4000000 | tf_op jit(solution)/shard_map/pallas_call | solution.py:266
  6.5 3.3 %collective-permute-start.13 = (bf16[128,1024]{1,0:T(8,128)(2,1)S(1)}, bf16[128,1024]{1,0:T(8,128)(2,1)S(1)}, u32[]{:S(2)}, u32[]{:S(2)}) collective-permute-start(bf16[128,1024]{1,0:T(8,128)(2,1)S(1)} %get-tuple-element.24.refs_0_), channel_id=1, source_target_pairs={{4,0},{8,4},{12,8},{0,12},{5,1},{9,5},{13,9},{1,13},{6,2},{10,6},{... | collective-permute-start | bytes 786440 | tf_op jit(solution)/shard_map/ppermute | solution.py:256
  9.8 1.9 %copy.12 = bf16[16,4,4,16,128]{4,3,2,1,0:T(8,128)(2,1)S(1)} copy(bf16[16,4,4,16,128]{4,0,1,3,2:T(8,128)(2,1)} %bitcast.24) | data formatting | bytes 2097152 | tf_op jit(solution)/shard_map/transpose | solution.py:288
  11.8 0.8 %copy-done.2 = bf16[4,16,16,128]{3,2,1,0:T(8,128)(2,1)S(1)} copy-done((bf16[4,16,16,128]{3,2,1,0:T(8,128)(2,1)S(1)}, bf16[4,16,16,128]{3,2,1,0:T(8,128)(2,1)}, u32[]{:S(2)}) %copy-start.2) | copy-done | bytes 262168
  12.7 2.7 %shard_map.102 = (f32[8,128,128]{2,1,0:T(8,128)S(1)}, f32[4,128,128]{2,1,0:T(8,128)S(1)}, f32[4,128,128]{2,1,0:T(8,128)S(1)}) custom-call(s32[4,4]{1,0:T(4,128)S(1)} %copy-done.3, s32[1]{0:T(128)} %bitcast.2.base_ref, bf16[16,256,128]{2,1,0:T(8,128)(2,1)S(1)} %bitcast.18, bf16[16,64,128]{2,1,0:T(8,128)(2,1)S(1)} %bitcast.20, ...), custom_call_target="tpu_custom_call" | custom-call | flops 1000000000 | bytes 4000000 | tf_op jit(solution)/shard_map/pallas_call | solution.py:266
  15.4 0.8 %dynamic-slice_bitcast_fusion.w1_ref = bf16[128,64]{1,0:T(8,128)(2,1)S(1)} fusion(bf16[4,128,64]{2,1,0:T(8,128)(2,1)} %constant.20.clone, s32[]{:T(128)S(6)} %select_n.4), kind=kLoop, calls=%fused_computation | loop fusion | bytes 32772 | tf_op jit(solution)/shard_map/jit(dynamic_index_in_dim)/squeeze | solution.py:305
  16.2 3.3 %collective-permute-start.5 = (bf16[128,512]{1,0:T(8,128)(2,1)S(1)}, bf16[128,512]{1,0:T(8,128)(2,1)S(1)}, u32[]{:S(2)}, u32[]{:S(2)}) collective-permute-start(bf16[128,512]{1,0:T(8,128)(2,1)S(1)} %get-tuple-element.25.refs_2_), channel_id=1, source_target_pairs={{4,0},{8,4},{12,8},{0,12},{5,1},{9,5},{13,9},{1,13},{6,2},{10,6},{... | collective-permute-start | bytes 393224 | tf_op jit(solution)/shard_map/ppermute | solution.py:256
  19.5 1.9 %shard_map.100.g_ref = bf16[8,256,256]{2,1,0:T(8,128)(2,1)S(1)} custom-call(s32[4,4]{1,0:T(4,128)S(1)} %copy-done.3, s32[1]{0:T(128)} %bitcast.2.base_ref, bf16[16,256,128]{2,1,0:T(8,128)(2,1)S(1)} %bitcast.19, bf16[4,16,16,128]{3,2,1,0:T(8,128)(2,1)S(1)} %collective-permute-done.a_ref, bf16[4,16,16,128]{3,2,1,0:T(8,128)(2,1)S(1)} %collective-permute-done.1.b_ref), custom_call_target="tpu_custom_call" | custom-call | flops 1000000000 | bytes 4000000 | tf_op jit(solution)/shard_map/pallas_call | solution.py:266
  21.7 3.0 %collective-permute-start.3 = (bf16[128,512]{1,0:T(8,128)(2,1)S(1)}, bf16[128,512]{1,0:T(8,128)(2,1)S(1)}, u32[]{:S(2)}, u32[]{:S(2)}) collective-permute-start(bf16[128,512]{1,0:T(8,128)(2,1)S(1)} %get-tuple-element.23.refs_1_), channel_id=1, source_target_pairs={{4,0},{8,4},{12,8},{0,12},{5,1},{9,5},{13,9},{1,13},{6,2},{10,6},{... | collective-permute-start | bytes 393224 | tf_op jit(solution)/shard_map/ppermute | solution.py:256
  24.7 2.1 %collective-permute-done.13.b_ref = bf16[128,1024]{1,0:T(8,128)(2,1)S(1)} collective-permute-done((bf16[128,1024]{1,0:T(8,128)(2,1)S(1)}, bf16[128,1024]{1,0:T(8,128)(2,1)S(1)}, u32[]{:S(2)}, u32[]{:S(2)}) %collective-permute-start.13) | collective-permute-done | bytes 262176 | tf_op jit(solution)/shard_map/ppermute | solution.py:256
  26.8 0.5 %shard_map.105 = (bf16[4,4,16,128]{3,2,1,0:T(8,128)(2,1)S(1)}, bf16[4,4,16,128]{3,2,1,0:T(8,128)(2,1)S(1)}, bf16[4,4,16,128]{3,2,1,0:T(8,128)(2,1)S(1)}, bf16[4,4,16,128]{3,2,1,0:T(8,128)(2,1)S(1)}) custom-call(s32[1]{0:T(128)} %bitcast.1.me_ref, bf16[8,256,256]{2,1,0:T(8,128)(2,1)S(1)} %shard_map.100.g_ref, ...), custom_call_target="tpu_custom_call" | custom-call | flops 1000000000 | bytes 4000000 | tf_op jit(solution)/shard_map/pallas_call | solution.py:266
  27.4 5.7 %collective-permute-start.14 = (bf16[4,4,16,128]{3,2,1,0:T(8,128)(2,1)S(1)}, bf16[4,4,16,128]{3,2,1,0:T(8,128)(2,1)S(1)}, u32[]{:S(2)}, u32[]{:S(2)}) collective-permute-start(bf16[4,4,16,128]{3,2,1,0:T(8,128)(2,1)S(1)} %get-tuple-element.38), channel_id=1, source_target_pairs={{0,1},{1,2},{2,3},{3,0},{4,5},{5,6},{6,7},{7,4},{8,9},{9,10},{10,1... | collective-permute-start | bytes 196616 | tf_op jit(solution)/shard_map/ppermute | solution.py:321
  33.3 1.7 %collective-permute-start.16 = (bf16[4,4,16,128]{3,2,1,0:T(8,128)(2,1)S(1)}, bf16[4,4,16,128]{3,2,1,0:T(8,128)(2,1)S(1)}, u32[]{:S(2)}, u32[]{:S(2)}) collective-permute-start(bf16[4,4,16,128]{3,2,1,0:T(8,128)(2,1)S(1)} %get-tuple-element.40), channel_id=1, source_target_pairs={{0,3},{1,0},{2,1},{3,2},{4,7},{5,4},{6,5},{7,6},{8,11},{9,8},{10,9... | collective-permute-start | bytes 196616 | tf_op jit(solution)/shard_map/ppermute | solution.py:321
  35.3 0.5 %collective-permute-done.2.a_ref = bf16[128,512]{1,0:T(8,128)(2,1)S(1)} collective-permute-done((bf16[128,512]{1,0:T(8,128)(2,1)S(1)}, bf16[128,512]{1,0:T(8,128)(2,1)S(1)}, u32[]{:S(2)}, u32[]{:S(2)}) %collective-permute-start.2) | collective-permute-done | bytes 131104 | tf_op jit(solution)/shard_map/ppermute | solution.py:256
  35.8 2.1 %collective-permute-start.11 = (bf16[4,4,8,128]{3,2,1,0:T(8,128)(2,1)S(1)}, bf16[4,4,8,128]{3,2,1,0:T(8,128)(2,1)S(1)}, u32[]{:S(2)}, u32[]{:S(2)}) collective-permute-start(bf16[4,4,8,128]{3,2,1,0:T(8,128)(2,1)S(1)} %get-tuple-element.35), channel_id=1, source_target_pairs={{0,3},{1,0},{2,1},{3,2},{4,7},{5,4},{6,5},{7,6},{8,11},{9,8},{10,9... | collective-permute-start | bytes 98312 | tf_op jit(solution)/shard_map/ppermute | solution.py:321
  38.1 2.2 %collective-permute-start.7 = (bf16[4,4,8,128]{3,2,1,0:T(8,128)(2,1)S(1)}, bf16[4,4,8,128]{3,2,1,0:T(8,128)(2,1)S(1)}, u32[]{:S(2)}, u32[]{:S(2)}) collective-permute-start(bf16[4,4,8,128]{3,2,1,0:T(8,128)(2,1)S(1)} %get-tuple-element.31), channel_id=1, source_target_pairs={{0,1},{1,2},{2,3},{3,0},{4,5},{5,6},{6,7},{7,4},{8,9},{9,10},{10,1... | collective-permute-start | bytes 98312 | tf_op jit(solution)/shard_map/ppermute | solution.py:321
  41.2 1.5 %collective-permute-start.6 = (bf16[4,4,8,128]{3,2,1,0:T(8,128)(2,1)S(1)}, bf16[4,4,8,128]{3,2,1,0:T(8,128)(2,1)S(1)}, u32[]{:S(2)}, u32[]{:S(2)}) collective-permute-start(bf16[4,4,8,128]{3,2,1,0:T(8,128)(2,1)S(1)} %get-tuple-element.30), channel_id=1, source_target_pairs={{0,1},{1,2},{2,3},{3,0},{4,5},{5,6},{6,7},{7,4},{8,9},{9,10},{10,1... | collective-permute-start | bytes 98312 | tf_op jit(solution)/shard_map/ppermute | solution.py:321
  42.7 1.3 %collective-permute-start.8 = (bf16[4,4,8,128]{3,2,1,0:T(8,128)(2,1)S(1)}, bf16[4,4,8,128]{3,2,1,0:T(8,128)(2,1)S(1)}, u32[]{:S(2)}, u32[]{:S(2)}) collective-permute-start(bf16[4,4,8,128]{3,2,1,0:T(8,128)(2,1)S(1)} %get-tuple-element.32), channel_id=1, source_target_pairs={{0,2},{1,3},{2,0},{3,1},{4,6},{5,7},{6,4},{7,5},{8,10},{9,11},{10,... | collective-permute-start | bytes 98312 | tf_op jit(solution)/shard_map/ppermute | solution.py:321
  44.0 1.5 %time.2.refs_8_ = bf16[4,4,2,64,128]{4,3,2,1,0:T(8,128)(2,1)} custom-call(bf16[128,64]{1,0:T(8,128)(2,1)S(1)} %dynamic-slice_bitcast_fusion.w1_ref, f32[2,32,128]{2,1,0:T(8,128)S(1)} %copy-done.6, bf16[512,256]{1,0:T(8,128)(2,1)S(1)} %copy-done.5, bf16[4,4,16,128]{3,2,1,0:T(8,128)(2,1)S(1)} %get-tuple-element.37.refs_0_, ...), custom_call_target="tpu_custom_call" | custom-call | flops 1000000000 | bytes 2000000 | tf_op jit(solution)/shard_map/time/pallas_call | solution.py:329
  46.0 1.5 %time.3 = bf16[4,4,2,64,128]{4,3,2,1,0:T(8,128)(2,1)} custom-call(bf16[128,64]{1,0:T(8,128)(2,1)S(1)} %dynamic-slice_bitcast_fusion.w1_ref, f32[2,32,128]{2,1,0:T(8,128)S(1)} %copy-done.6, bf16[512,256]{1,0:T(8,128)(2,1)S(1)} %copy-done.5, bf16[4,4,8,128]{3,2,1,0:T(8,128)(2,1)S(1)} %get-tuple-element.27.refs_0_, ...), custom_call_target="tpu_custom_call", output_to_operand_aliasing={{}: (11, {})} | custom-call | flops 1000000000 | bytes 2000000 | tf_op jit(solution)/shard_map/time/pallas_call | solution.py:329
  (37 shorter events, 2.6 us)
Async XLA Ops:
  0.0 16.2 %collective-permute-start = (bf16[4,16,16,128]{3,2,1,0:T(8,128)(2,1)}, bf16[4,16,16,128]{3,2,1,0:T(8,128)(2,1)S(1)}, u32[]{:S(2)}, u32[]{:S(2)}) collective-permute-start(bf16[4,16,16,128]{3,2,1,0:T(8,128)(2,1)} %p_ref.1), channel_id=1, source_target_pairs={{0,4},{4,8},{8,12},{12,0},{1,5},{5,9},{9,13},{13,1},{2,6},{6,10},{... | collective-permute-start | bytes 786440 | tf_op jit(solution)/shard_map/ppermute | solution.py:256
  2.1 17.4 %collective-permute-start.1 = (bf16[4,16,16,128]{3,2,1,0:T(8,128)(2,1)}, bf16[4,16,16,128]{3,2,1,0:T(8,128)(2,1)S(1)}, u32[]{:S(2)}, u32[]{:S(2)}) collective-permute-start(bf16[4,16,16,128]{3,2,1,0:T(8,128)(2,1)} %p_ref.1), channel_id=1, source_target_pairs={{4,0},{8,4},{12,8},{0,12},{5,1},{9,5},{13,9},{1,13},{6,2},{10,6},{... | collective-permute-start | bytes 786440 | tf_op jit(solution)/shard_map/ppermute | solution.py:256
  4.1 1.0 %copy-start = (bf16[4,2,32,1024]{3,2,1,0:T(8,128)(2,1)S(1)}, bf16[4,2,32,1024]{3,2,1,0:T(8,128)(2,1)}, u32[]{:S(2)}) copy-start(bf16[4,2,32,1024]{3,2,1,0:T(8,128)(2,1)} %x_ref.1) | copy-start | bytes 1572868
  6.5 15.2 %collective-permute-start.12 = (bf16[128,1024]{1,0:T(8,128)(2,1)S(1)}, bf16[128,1024]{1,0:T(8,128)(2,1)S(1)}, u32[]{:S(2)}, u32[]{:S(2)}) collective-permute-start(bf16[128,1024]{1,0:T(8,128)(2,1)S(1)} %get-tuple-element.24.refs_0_), channel_id=1, source_target_pairs={{0,4},{4,8},{8,12},{12,0},{1,5},{5,9},{9,13},{13,1},{2,6},{6,10},{... | collective-permute-start | bytes 786440 | tf_op jit(solution)/shard_map/ppermute | solution.py:256
  6.5 20.3 %collective-permute-start.13 = (bf16[128,1024]{1,0:T(8,128)(2,1)S(1)}, bf16[128,1024]{1,0:T(8,128)(2,1)S(1)}, u32[]{:S(2)}, u32[]{:S(2)}) collective-permute-start(bf16[128,1024]{1,0:T(8,128)(2,1)S(1)} %get-tuple-element.24.refs_0_), channel_id=1, source_target_pairs={{4,0},{8,4},{12,8},{0,12},{5,1},{9,5},{13,9},{1,13},{6,2},{10,6},{... | collective-permute-start | bytes 786440 | tf_op jit(solution)/shard_map/ppermute | solution.py:256
  9.8 23.2 %collective-permute-start.4 = (bf16[128,512]{1,0:T(8,128)(2,1)S(1)}, bf16[128,512]{1,0:T(8,128)(2,1)S(1)}, u32[]{:S(2)}, u32[]{:S(2)}) collective-permute-start(bf16[128,512]{1,0:T(8,128)(2,1)S(1)} %get-tuple-element.25.refs_2_), channel_id=1, source_target_pairs={{0,4},{4,8},{8,12},{12,0},{1,5},{5,9},{9,13},{13,1},{2,6},{6,10},{... | collective-permute-start | bytes 393224 | tf_op jit(solution)/shard_map/ppermute | solution.py:256
  9.8 2.0 %copy-start.7 = (bf16[4,16,16,128]{3,2,1,0:T(8,128)(2,1)S(1)}, bf16[4,16,16,128]{3,2,1,0:T(8,128)(2,1)}, u32[]{:S(2)}) copy-start(bf16[4,16,16,128]{3,2,1,0:T(8,128)(2,1)} %param.13) | copy-start | bytes 786436
  11.7 1.0 %copy-start.2 = (bf16[4,16,16,128]{3,2,1,0:T(8,128)(2,1)S(1)}, bf16[4,16,16,128]{3,2,1,0:T(8,128)(2,1)}, u32[]{:S(2)}) copy-start(bf16[4,16,16,128]{3,2,1,0:T(8,128)(2,1)} %p_ref.1) | copy-start | bytes 786436
  11.8 0.9 %copy-start.3 = (s32[4,4]{1,0:T(4,128)S(1)}, s32[4,4]{1,0:T(4,128)}, u32[]{:S(2)}) copy-start(s32[4,4]{1,0:T(4,128)} %near_ref.3) | copy-start | bytes 196
  16.2 10.6 %copy-start.1 = (bf16[4,16,2,2,1024]{4,3,2,1,0:T(2,128)(2,1)S(1)}, bf16[4,16,2,2,1024]{4,3,2,1,0:T(2,128)(2,1)}, u32[]{:S(2)}) copy-start(bf16[4,16,2,2,1024]{4,3,2,1,0:T(2,128)(2,1)} %param.16) | copy-start | bytes 1572868
  16.2 17.1 %collective-permute-start.5 = (bf16[128,512]{1,0:T(8,128)(2,1)S(1)}, bf16[128,512]{1,0:T(8,128)(2,1)S(1)}, u32[]{:S(2)}, u32[]{:S(2)}) collective-permute-start(bf16[128,512]{1,0:T(8,128)(2,1)S(1)} %get-tuple-element.25.refs_2_), channel_id=1, source_target_pairs={{4,0},{8,4},{12,8},{0,12},{5,1},{9,5},{13,9},{1,13},{6,2},{10,6},{... | collective-permute-start | bytes 393224 | tf_op jit(solution)/shard_map/ppermute | solution.py:256
  19.5 16.3 %collective-permute-start.2 = (bf16[128,512]{1,0:T(8,128)(2,1)S(1)}, bf16[128,512]{1,0:T(8,128)(2,1)S(1)}, u32[]{:S(2)}, u32[]{:S(2)}) collective-permute-start(bf16[128,512]{1,0:T(8,128)(2,1)S(1)} %get-tuple-element.23.refs_1_), channel_id=1, source_target_pairs={{0,4},{4,8},{8,12},{12,0},{1,5},{5,9},{9,13},{13,1},{2,6},{6,10},{... | collective-permute-start | bytes 393224 | tf_op jit(solution)/shard_map/ppermute | solution.py:256
  21.7 16.4 %collective-permute-start.3 = (bf16[128,512]{1,0:T(8,128)(2,1)S(1)}, bf16[128,512]{1,0:T(8,128)(2,1)S(1)}, u32[]{:S(2)}, u32[]{:S(2)}) collective-permute-start(bf16[128,512]{1,0:T(8,128)(2,1)S(1)} %get-tuple-element.23.refs_1_), channel_id=1, source_target_pairs={{4,0},{8,4},{12,8},{0,12},{5,1},{9,5},{13,9},{1,13},{6,2},{10,6},{... | collective-permute-start | bytes 393224 | tf_op jit(solution)/shard_map/ppermute | solution.py:256
  27.4 13.5 %collective-permute-start.14 = (bf16[4,4,16,128]{3,2,1,0:T(8,128)(2,1)S(1)}, bf16[4,4,16,128]{3,2,1,0:T(8,128)(2,1)S(1)}, u32[]{:S(2)}, u32[]{:S(2)}) collective-permute-start(bf16[4,4,16,128]{3,2,1,0:T(8,128)(2,1)S(1)} %get-tuple-element.38), channel_id=1, source_target_pairs={{0,1},{1,2},{2,3},{3,0},{4,5},{5,6},{6,7},{7,4},{8,9},{9,10},{10,1... | collective-permute-start | bytes 196616 | tf_op jit(solution)/shard_map/ppermute | solution.py:321
  33.0 8.1 %collective-permute-start.15 = (bf16[4,4,16,128]{3,2,1,0:T(8,128)(2,1)S(1)}, bf16[4,4,16,128]{3,2,1,0:T(8,128)(2,1)S(1)}, u32[]{:S(2)}, u32[]{:S(2)}) collective-permute-start(bf16[4,4,16,128]{3,2,1,0:T(8,128)(2,1)S(1)} %get-tuple-element.39), channel_id=1, source_target_pairs={{0,2},{1,3},{2,0},{3,1},{4,6},{5,7},{6,4},{7,5},{8,10},{9,11},{10,... | collective-permute-start | bytes 196616 | tf_op jit(solution)/shard_map/ppermute | solution.py:321
  33.3 9.4 %collective-permute-start.16 = (bf16[4,4,16,128]{3,2,1,0:T(8,128)(2,1)S(1)}, bf16[4,4,16,128]{3,2,1,0:T(8,128)(2,1)S(1)}, u32[]{:S(2)}, u32[]{:S(2)}) collective-permute-start(bf16[4,4,16,128]{3,2,1,0:T(8,128)(2,1)S(1)} %get-tuple-element.40), channel_id=1, source_target_pairs={{0,3},{1,0},{2,1},{3,2},{4,7},{5,4},{6,5},{7,6},{8,11},{9,8},{10,9... | collective-permute-start | bytes 196616 | tf_op jit(solution)/shard_map/ppermute | solution.py:321
  35.8 4.9 %collective-permute-start.11 = (bf16[4,4,8,128]{3,2,1,0:T(8,128)(2,1)S(1)}, bf16[4,4,8,128]{3,2,1,0:T(8,128)(2,1)S(1)}, u32[]{:S(2)}, u32[]{:S(2)}) collective-permute-start(bf16[4,4,8,128]{3,2,1,0:T(8,128)(2,1)S(1)} %get-tuple-element.35), channel_id=1, source_target_pairs={{0,3},{1,0},{2,1},{3,2},{4,7},{5,4},{6,5},{7,6},{8,11},{9,8},{10,9... | collective-permute-start | bytes 98312 | tf_op jit(solution)/shard_map/ppermute | solution.py:321
  38.1 7.4 %collective-permute-start.7 = (bf16[4,4,8,128]{3,2,1,0:T(8,128)(2,1)S(1)}, bf16[4,4,8,128]{3,2,1,0:T(8,128)(2,1)S(1)}, u32[]{:S(2)}, u32[]{:S(2)}) collective-permute-start(bf16[4,4,8,128]{3,2,1,0:T(8,128)(2,1)S(1)} %get-tuple-element.31), channel_id=1, source_target_pairs={{0,1},{1,2},{2,3},{3,0},{4,5},{5,6},{6,7},{7,4},{8,9},{9,10},{10,1... | collective-permute-start | bytes 98312 | tf_op jit(solution)/shard_map/ppermute | solution.py:321
  40.2 3.7 %copy-start.5 = (bf16[512,256]{1,0:T(8,128)(2,1)S(1)}, bf16[512,256]{1,0:T(8,128)(2,1)}, u32[]{:S(2)}) copy-start(bf16[512,256]{1,0:T(8,128)(2,1)} %constant.22.clone.w2_ref) | copy-start | bytes 786436
  40.2 3.7 %copy-start.6 = (f32[2,32,128]{2,1,0:T(8,128)S(1)}, f32[2,32,128]{2,1,0:T(8,128)}, u32[]{:S(2)}) copy-start(f32[2,32,128]{2,1,0:T(8,128)} %constant.21.clone.tw_ref) | copy-start | bytes 98308
  40.7 4.7 %collective-permute-start.9 = (bf16[4,4,8,128]{3,2,1,0:T(8,128)(2,1)S(1)}, bf16[4,4,8,128]{3,2,1,0:T(8,128)(2,1)S(1)}, u32[]{:S(2)}, u32[]{:S(2)}) collective-permute-start(bf16[4,4,8,128]{3,2,1,0:T(8,128)(2,1)S(1)} %get-tuple-element.33), channel_id=1, source_target_pairs={{0,2},{1,3},{2,0},{3,1},{4,6},{5,7},{6,4},{7,5},{8,10},{9,11},{10,... | collective-permute-start | bytes 98312 | tf_op jit(solution)/shard_map/ppermute | solution.py:321
  40.9 4.6 %collective-permute-start.10 = (bf16[4,4,8,128]{3,2,1,0:T(8,128)(2,1)S(1)}, bf16[4,4,8,128]{3,2,1,0:T(8,128)(2,1)S(1)}, u32[]{:S(2)}, u32[]{:S(2)}) collective-permute-start(bf16[4,4,8,128]{3,2,1,0:T(8,128)(2,1)S(1)} %get-tuple-element.34), channel_id=1, source_target_pairs={{0,3},{1,0},{2,1},{3,2},{4,7},{5,4},{6,5},{7,6},{8,11},{9,8},{10,9... | collective-permute-start | bytes 98312 | tf_op jit(solution)/shard_map/ppermute | solution.py:321
  41.2 4.3 %collective-permute-start.6 = (bf16[4,4,8,128]{3,2,1,0:T(8,128)(2,1)S(1)}, bf16[4,4,8,128]{3,2,1,0:T(8,128)(2,1)S(1)}, u32[]{:S(2)}, u32[]{:S(2)}) collective-permute-start(bf16[4,4,8,128]{3,2,1,0:T(8,128)(2,1)S(1)} %get-tuple-element.30), channel_id=1, source_target_pairs={{0,1},{1,2},{2,3},{3,0},{4,5},{5,6},{6,7},{7,4},{8,9},{9,10},{10,1... | collective-permute-start | bytes 98312 | tf_op jit(solution)/shard_map/ppermute | solution.py:321
  42.7 3.3 %collective-permute-start.8 = (bf16[4,4,8,128]{3,2,1,0:T(8,128)(2,1)S(1)}, bf16[4,4,8,128]{3,2,1,0:T(8,128)(2,1)S(1)}, u32[]{:S(2)}, u32[]{:S(2)}) collective-permute-start(bf16[4,4,8,128]{3,2,1,0:T(8,128)(2,1)S(1)} %get-tuple-element.32), channel_id=1, source_target_pairs={{0,2},{1,3},{2,0},{3,1},{4,6},{5,7},{6,4},{7,5},{8,10},{9,11},{10,... | collective-permute-start | bytes 98312 | tf_op jit(solution)/shard_map/ppermute | solution.py:321
  (1 other events, 0.7 us)
where the time goes:
time: 48.4 us; the launch traced here: 47.4 us
  starting transfers between devices  28.8 us (60%)
  Pallas kernels  9.35 us (19%)
  local copies, waits for them, and re-layouts  5.35 us (11%)
  waiting for transfers between devices  3.74 us (8%)
    ppermute x9, starting transfers between devices, body(): lax.ppermute(sent[d], 'sc', [(i, i ^ d if [0, 0, 0][at] else (i + d) % pa...  15.1 us
    ppermute x8, starting transfers between devices, both_ways(): moved.append(lax.ppermute(x, 'cell', pairs))  13.8 us
    pallas_call x6, Pallas kernels, call(): pl.pallas_call(kernel, in_specs=[smem] * scalars + [vmem] * (len(ins) - s...  6.42 us
    ppermute x8, waiting for transfers between devices, both_ways(): moved.append(lax.ppermute(x, 'cell', pairs))  3.08 us
    pallas_call x2, Pallas kernels, body(): pl.pallas_call(functools.partial(time_kernel, t, halves), in_specs=[vmem]...  2.93 us
    unnamed x16, local copies, waits for them, and re-layouts  2.57 us
    transpose x1, local copies, waits for them, and re-layouts, body(): cross_channel.transpose(3, 2, 0, 1, 4)  1.95 us
  transfers between devices with their start and end apart: 17, of which 6 were waited for; matrix products, arithmetic and copies ran while one was open for 6% of the time, Pallas kernels for 17%

commit v1 on v0

--- a/solution.py
+++ b/solution.py
@@ -170,8 +170,7 @@
     per = LANES // rows
     w1 = w1_ref[...]
     w2 = w2_ref[...]
-    n2 = w2.shape[0] // 2
-    tall = n2 // per
+    tall = w2.shape[0] // per
     batch = min(seqs, 2 * per)
     held_as = BF16 if halves == 1 else F32
     copies = []
@@ -182,7 +181,6 @@
         ]
         data = jnp.concatenate(data, axis=1).astype(BF16)
         both = jnp.dot(w1, data, preferred_element_type=F32)
-        both = both[: 2 * rows] + both[2 * rows :]
         turned = []
         for q in range(batch):
             re = both[:rows, q * LANES : (q + 1) * LANES]
@@ -191,10 +189,7 @@
                 jnp.concatenate([re * tw_ref[0] - im * tw_ref[1], re * tw_ref[1] + im * tw_ref[0]], axis=1)
             )
         turned = jnp.concatenate(turned, axis=0)
-        high = turned.astype(BF16)
-        low = (turned - high.astype(F32)).astype(BF16)
-        prod = lax.dot_general(w2, high, NT, preferred_element_type=F32)
-        prod = prod[:n2] + prod[n2:] + lax.dot_general(w2[:n2], low, NT, preferred_element_type=F32)
+        prod = lax.dot_general(w2, turned.astype(BF16), NT, preferred_element_type=F32)
         for quad in range(batch // per):
             lanes = slice(quad * LANES, (quad + 1) * LANES)
             pieces = swap_groups([prod[i * tall : (i + 1) * tall, lanes].astype(BF16) for i in range(per)], rows)
@@ -212,12 +207,6 @@
     return np.block([[np.cos(angle), -np.sin(angle)], [np.sin(angle), np.cos(angle)]])
 
 
-def split_rows(table):
-    high = table.astype(jnp.bfloat16)
-    low = (table - high.astype(np.float64)).astype(jnp.bfloat16)
-    return np.concatenate([high, low], axis=0)
-
-
 def tables(length, parts):
     rows = length // LANES
     local = rows // parts
@@ -228,14 +217,14 @@
         order = np.concatenate([src * local + np.arange(local) for src in source])
         angle = 2 * np.pi * (np.outer(m, order) % rows) / rows
         full = rotation(angle).reshape(2 * rows, 2, rows).transpose(0, 2, 1).reshape(2 * rows, 2 * rows)
-        w1.append(split_rows(full))
+        w1.append(full.astype(jnp.bfloat16))
     lane = np.arange(LANES)
     angle = 2 * np.pi * (np.outer(m, lane) % length) / length
     twist = (np.stack([np.cos(angle), np.sin(angle)]) / math.sqrt(length)).astype(np.float32)
     per = LANES // rows
     angle = 2 * np.pi * (np.outer(lane, lane) % LANES) / LANES
     w2 = rotation(angle).reshape(2, rows, per, 2 * LANES).transpose(2, 1, 0, 3).reshape(2 * LANES, 2 * LANES)
-    return np.stack(w1), twist, split_rows(w2)
+    return np.stack(w1), twist, w2.astype(jnp.bfloat16)
 
 
 def body(symbols, precoders, plan, own_channel, cross_channel, neighbours, noise):

time: 48.4 us -> 48.2 us (level)
  transfers between devices with their start and end apart: 17 -> 17, of which waited for: 6 -> 6; matrix products, arithmetic and copies ran while one was open for 6% -> 6% of each run, Pallas kernels for 17% -> 16%
where the time goes in v1:
time: 48.2 us; the launch traced here: 47.2 us
  starting transfers between devices  28.8 us (60%)
  Pallas kernels  8.97 us (19%)
  local copies, waits for them, and re-layouts  5.31 us (11%)
  waiting for transfers between devices  4.01 us (8%)
    ppermute x9, starting transfers between devices, body(): lax.ppermute(sent[d], 'sc', [(i, i ^ d if [0, 0, 0][at] else (i + d) % pa...  15.1 us
    ppermute x8, starting transfers between devices, both_ways(): moved.append(lax.ppermute(x, 'cell', pairs))  13.7 us
    pallas_call x6, Pallas kernels, call(): pl.pallas_call(kernel, in_specs=[smem] * scalars + [vmem] * (len(ins) - s...  6.42 us
    ppermute x8, waiting for transfers between devices, both_ways(): moved.append(lax.ppermute(x, 'cell', pairs))  3.17 us
    unnamed x16, local copies, waits for them, and re-layouts  2.57 us
    pallas_call x2, Pallas kernels, body(): pl.pallas_call(functools.partial(time_kernel, t, halves), in_specs=[vmem]...  2.55 us
    transpose x1, local copies, waits for them, and re-layouts, body(): cross_channel.transpose(3, 2, 0, 1, 4)  1.95 us
  transfers between devices with their start and end apart: 17, of which 6 were waited for; matrix products, arithmetic and copies ran while one was open for 6% of the time, Pallas kernels for 16%

profile of v1, /device:TPU:1, one launch (start us, length us, event | category | flops | bytes accessed | tf_op | source)
XLA Modules:
  0.0 47.2 jit_solution(2435768423917581520)
XLA Ops:
  0.0 2.1 %collective-permute-start = (bf16[4,16,16,128]{3,2,1,0:T(8,128)(2,1)}, bf16[4,16,16,128]{3,2,1,0:T(8,128)(2,1)S(1)}, u32[]{:S(2)}, u32[]{:S(2)}) collective-permute-start(bf16[4,16,16,128]{3,2,1,0:T(8,128)(2,1)} %p_ref.1), channel_id=1, source_target_pairs={{0,4},{4,8},{8,12},{12,0},{1,5},{5,9},{9,13},{13,1},{2,6},{6,10},{... | collective-permute-start | bytes 786440 | tf_op jit(solution)/shard_map/ppermute | solution.py:245
  2.1 2.0 %collective-permute-start.1 = (bf16[4,16,16,128]{3,2,1,0:T(8,128)(2,1)}, bf16[4,16,16,128]{3,2,1,0:T(8,128)(2,1)S(1)}, u32[]{:S(2)}, u32[]{:S(2)}) collective-permute-start(bf16[4,16,16,128]{3,2,1,0:T(8,128)(2,1)} %p_ref.1), channel_id=1, source_target_pairs={{4,0},{8,4},{12,8},{0,12},{5,1},{9,5},{13,9},{1,13},{6,2},{10,6},{... | collective-permute-start | bytes 786440 | tf_op jit(solution)/shard_map/ppermute | solution.py:245
  4.1 1.0 %copy-done = bf16[4,2,32,1024]{3,2,1,0:T(8,128)(2,1)S(1)} copy-done((bf16[4,2,32,1024]{3,2,1,0:T(8,128)(2,1)S(1)}, bf16[4,2,32,1024]{3,2,1,0:T(8,128)(2,1)}, u32[]{:S(2)}) %copy-start) | copy-done | bytes 524312
  5.2 0.7 %copy-done.4 = s32[4]{0:T(128)S(1)} copy-done((s32[4]{0:T(128)S(1)}, s32[4]{0:T(128)}, u32[]{:S(2)}) %copy-start.4) | copy-done | bytes 40
  5.8 0.6 %shard_map.101 = (bf16[128,1024]{1,0:T(8,128)(2,1)S(1)}, bf16[128,512]{1,0:T(8,128)(2,1)S(1)}, bf16[128,512]{1,0:T(8,128)(2,1)S(1)}) custom-call(s32[4]{0:T(128)S(1)} %copy-done.4, bf16[4,2,32,1024]{3,2,1,0:T(8,128)(2,1)S(1)} %copy-done), custom_call_target="tpu_custom_call" | custom-call | flops 1000000000 | bytes 4000000 | tf_op jit(solution)/shard_map/pallas_call | solution.py:255
  6.5 3.3 %collective-permute-start.13 = (bf16[128,1024]{1,0:T(8,128)(2,1)S(1)}, bf16[128,1024]{1,0:T(8,128)(2,1)S(1)}, u32[]{:S(2)}, u32[]{:S(2)}) collective-permute-start(bf16[128,1024]{1,0:T(8,128)(2,1)S(1)} %get-tuple-element.24.refs_0_), channel_id=1, source_target_pairs={{4,0},{8,4},{12,8},{0,12},{5,1},{9,5},{13,9},{1,13},{6,2},{10,6},{... | collective-permute-start | bytes 786440 | tf_op jit(solution)/shard_map/ppermute | solution.py:245
  9.8 1.9 %copy.12 = bf16[16,4,4,16,128]{4,3,2,1,0:T(8,128)(2,1)S(1)} copy(bf16[16,4,4,16,128]{4,0,1,3,2:T(8,128)(2,1)} %bitcast.24) | data formatting | bytes 2097152 | tf_op jit(solution)/shard_map/transpose | solution.py:277
  11.8 0.8 %copy-done.2 = bf16[4,16,16,128]{3,2,1,0:T(8,128)(2,1)S(1)} copy-done((bf16[4,16,16,128]{3,2,1,0:T(8,128)(2,1)S(1)}, bf16[4,16,16,128]{3,2,1,0:T(8,128)(2,1)}, u32[]{:S(2)}) %copy-start.2) | copy-done | bytes 262168
  12.7 2.7 %shard_map.102 = (f32[8,128,128]{2,1,0:T(8,128)S(1)}, f32[4,128,128]{2,1,0:T(8,128)S(1)}, f32[4,128,128]{2,1,0:T(8,128)S(1)}) custom-call(s32[4,4]{1,0:T(4,128)S(1)} %copy-done.3, s32[1]{0:T(128)} %bitcast.2.base_ref, bf16[16,256,128]{2,1,0:T(8,128)(2,1)S(1)} %bitcast.18, bf16[16,64,128]{2,1,0:T(8,128)(2,1)S(1)} %bitcast.20, ...), custom_call_target="tpu_custom_call" | custom-call | flops 1000000000 | bytes 4000000 | tf_op jit(solution)/shard_map/pallas_call | solution.py:255
  15.4 0.7 %dynamic-slice_bitcast_fusion.w1_ref = bf16[64,64]{1,0:T(8,128)(2,1)S(1)} fusion(bf16[4,64,64]{2,1,0:T(8,128)(2,1)} %constant.20.clone, s32[]{:T(128)S(6)} %select_n.4), kind=kLoop, calls=%fused_computation | loop fusion | bytes 16388 | tf_op jit(solution)/shard_map/jit(dynamic_index_in_dim)/squeeze | solution.py:294
  16.2 3.3 %collective-permute-start.5 = (bf16[128,512]{1,0:T(8,128)(2,1)S(1)}, bf16[128,512]{1,0:T(8,128)(2,1)S(1)}, u32[]{:S(2)}, u32[]{:S(2)}) collective-permute-start(bf16[128,512]{1,0:T(8,128)(2,1)S(1)} %get-tuple-element.25.refs_2_), channel_id=1, source_target_pairs={{4,0},{8,4},{12,8},{0,12},{5,1},{9,5},{13,9},{1,13},{6,2},{10,6},{... | collective-permute-start | bytes 393224 | tf_op jit(solution)/shard_map/ppermute | solution.py:245
  19.4 1.9 %shard_map.100.g_ref = bf16[8,256,256]{2,1,0:T(8,128)(2,1)S(1)} custom-call(s32[4,4]{1,0:T(4,128)S(1)} %copy-done.3, s32[1]{0:T(128)} %bitcast.2.base_ref, bf16[16,256,128]{2,1,0:T(8,128)(2,1)S(1)} %bitcast.19, bf16[4,16,16,128]{3,2,1,0:T(8,128)(2,1)S(1)} %collective-permute-done.a_ref, bf16[4,16,16,128]{3,2,1,0:T(8,128)(2,1)S(1)} %collective-permute-done.1.b_ref), custom_call_target="tpu_custom_call" | custom-call | flops 1000000000 | bytes 4000000 | tf_op jit(solution)/shard_map/pallas_call | solution.py:255
  21.7 3.0 %collective-permute-start.3 = (bf16[128,512]{1,0:T(8,128)(2,1)S(1)}, bf16[128,512]{1,0:T(8,128)(2,1)S(1)}, u32[]{:S(2)}, u32[]{:S(2)}) collective-permute-start(bf16[128,512]{1,0:T(8,128)(2,1)S(1)} %get-tuple-element.23.refs_1_), channel_id=1, source_target_pairs={{4,0},{8,4},{12,8},{0,12},{5,1},{9,5},{13,9},{1,13},{6,2},{10,6},{... | collective-permute-start | bytes 393224 | tf_op jit(solution)/shard_map/ppermute | solution.py:245
  24.7 2.2 %collective-permute-done.13.b_ref = bf16[128,1024]{1,0:T(8,128)(2,1)S(1)} collective-permute-done((bf16[128,1024]{1,0:T(8,128)(2,1)S(1)}, bf16[128,1024]{1,0:T(8,128)(2,1)S(1)}, u32[]{:S(2)}, u32[]{:S(2)}) %collective-permute-start.13) | collective-permute-done | bytes 262176 | tf_op jit(solution)/shard_map/ppermute | solution.py:245
  26.8 0.5 %shard_map.105 = (bf16[4,4,16,128]{3,2,1,0:T(8,128)(2,1)S(1)}, bf16[4,4,16,128]{3,2,1,0:T(8,128)(2,1)S(1)}, bf16[4,4,16,128]{3,2,1,0:T(8,128)(2,1)S(1)}, bf16[4,4,16,128]{3,2,1,0:T(8,128)(2,1)S(1)}) custom-call(s32[1]{0:T(128)} %bitcast.1.me_ref, bf16[8,256,256]{2,1,0:T(8,128)(2,1)S(1)} %shard_map.100.g_ref, ...), custom_call_target="tpu_custom_call" | custom-call | flops 1000000000 | bytes 4000000 | tf_op jit(solution)/shard_map/pallas_call | solution.py:255
  27.4 5.7 %collective-permute-start.14 = (bf16[4,4,16,128]{3,2,1,0:T(8,128)(2,1)S(1)}, bf16[4,4,16,128]{3,2,1,0:T(8,128)(2,1)S(1)}, u32[]{:S(2)}, u32[]{:S(2)}) collective-permute-start(bf16[4,4,16,128]{3,2,1,0:T(8,128)(2,1)S(1)} %get-tuple-element.38), channel_id=1, source_target_pairs={{0,1},{1,2},{2,3},{3,0},{4,5},{5,6},{6,7},{7,4},{8,9},{9,10},{10,1... | collective-permute-start | bytes 196616 | tf_op jit(solution)/shard_map/ppermute | solution.py:310
  33.3 1.7 %collective-permute-start.16 = (bf16[4,4,16,128]{3,2,1,0:T(8,128)(2,1)S(1)}, bf16[4,4,16,128]{3,2,1,0:T(8,128)(2,1)S(1)}, u32[]{:S(2)}, u32[]{:S(2)}) collective-permute-start(bf16[4,4,16,128]{3,2,1,0:T(8,128)(2,1)S(1)} %get-tuple-element.40), channel_id=1, source_target_pairs={{0,3},{1,0},{2,1},{3,2},{4,7},{5,4},{6,5},{7,6},{8,11},{9,8},{10,9... | collective-permute-start | bytes 196616 | tf_op jit(solution)/shard_map/ppermute | solution.py:310
  35.8 2.1 %collective-permute-start.11 = (bf16[4,4,8,128]{3,2,1,0:T(8,128)(2,1)S(1)}, bf16[4,4,8,128]{3,2,1,0:T(8,128)(2,1)S(1)}, u32[]{:S(2)}, u32[]{:S(2)}) collective-permute-start(bf16[4,4,8,128]{3,2,1,0:T(8,128)(2,1)S(1)} %get-tuple-element.35), channel_id=1, source_target_pairs={{0,3},{1,0},{2,1},{3,2},{4,7},{5,4},{6,5},{7,6},{8,11},{9,8},{10,9... | collective-permute-start | bytes 98312 | tf_op jit(solution)/shard_map/ppermute | solution.py:310
  38.1 2.2 %collective-permute-start.7 = (bf16[4,4,8,128]{3,2,1,0:T(8,128)(2,1)S(1)}, bf16[4,4,8,128]{3,2,1,0:T(8,128)(2,1)S(1)}, u32[]{:S(2)}, u32[]{:S(2)}) collective-permute-start(bf16[4,4,8,128]{3,2,1,0:T(8,128)(2,1)S(1)} %get-tuple-element.31), channel_id=1, source_target_pairs={{0,1},{1,2},{2,3},{3,0},{4,5},{5,6},{6,7},{7,4},{8,9},{9,10},{10,1... | collective-permute-start | bytes 98312 | tf_op jit(solution)/shard_map/ppermute | solution.py:310
  41.2 1.5 %collective-permute-start.6 = (bf16[4,4,8,128]{3,2,1,0:T(8,128)(2,1)S(1)}, bf16[4,4,8,128]{3,2,1,0:T(8,128)(2,1)S(1)}, u32[]{:S(2)}, u32[]{:S(2)}) collective-permute-start(bf16[4,4,8,128]{3,2,1,0:T(8,128)(2,1)S(1)} %get-tuple-element.30), channel_id=1, source_target_pairs={{0,1},{1,2},{2,3},{3,0},{4,5},{5,6},{6,7},{7,4},{8,9},{9,10},{10,1... | collective-permute-start | bytes 98312 | tf_op jit(solution)/shard_map/ppermute | solution.py:310
  42.7 1.3 %collective-permute-start.8 = (bf16[4,4,8,128]{3,2,1,0:T(8,128)(2,1)S(1)}, bf16[4,4,8,128]{3,2,1,0:T(8,128)(2,1)S(1)}, u32[]{:S(2)}, u32[]{:S(2)}) collective-permute-start(bf16[4,4,8,128]{3,2,1,0:T(8,128)(2,1)S(1)} %get-tuple-element.32), channel_id=1, source_target_pairs={{0,2},{1,3},{2,0},{3,1},{4,6},{5,7},{6,4},{7,5},{8,10},{9,11},{10,... | collective-permute-start | bytes 98312 | tf_op jit(solution)/shard_map/ppermute | solution.py:310
  44.0 1.3 %time.2.refs_8_ = bf16[4,4,2,64,128]{4,3,2,1,0:T(8,128)(2,1)} custom-call(bf16[64,64]{1,0:T(8,128)(2,1)S(1)} %dynamic-slice_bitcast_fusion.w1_ref, f32[2,32,128]{2,1,0:T(8,128)S(1)} %copy-done.6, bf16[256,256]{1,0:T(8,128)(2,1)S(1)} %copy-done.5, bf16[4,4,16,128]{3,2,1,0:T(8,128)(2,1)S(1)} %get-tuple-element.37.refs_0_, ...), custom_call_target="tpu_custom_call" | custom-call | flops 1000000000 | bytes 2000000 | tf_op jit(solution)/shard_map/time/pallas_call | solution.py:318
  45.3 0.7 %collective-permute-done.8.refs_4_ = bf16[4,4,8,128]{3,2,1,0:T(8,128)(2,1)S(1)} collective-permute-done((bf16[4,4,8,128]{3,2,1,0:T(8,128)(2,1)S(1)}, bf16[4,4,8,128]{3,2,1,0:T(8,128)(2,1)S(1)}, u32[]{:S(2)}, u32[]{:S(2)}) %collective-permute-start.8) | collective-permute-done | bytes 32800 | tf_op jit(solution)/shard_map/ppermute | solution.py:310
  46.0 1.3 %time.3 = bf16[4,4,2,64,128]{4,3,2,1,0:T(8,128)(2,1)} custom-call(bf16[64,64]{1,0:T(8,128)(2,1)S(1)} %dynamic-slice_bitcast_fusion.w1_ref, f32[2,32,128]{2,1,0:T(8,128)S(1)} %copy-done.6, bf16[256,256]{1,0:T(8,128)(2,1)S(1)} %copy-done.5, bf16[4,4,8,128]{3,2,1,0:T(8,128)(2,1)S(1)} %get-tuple-element.27.refs_0_, ...), custom_call_target="tpu_custom_call", output_to_operand_aliasing={{}: (11, {})} | custom-call | flops 1000000000 | bytes 2000000 | tf_op jit(solution)/shard_map/time/pallas_call | solution.py:318
  (37 shorter events, 2.7 us)
Async XLA Ops:
  0.0 16.2 %collective-permute-start = (bf16[4,16,16,128]{3,2,1,0:T(8,128)(2,1)}, bf16[4,16,16,128]{3,2,1,0:T(8,128)(2,1)S(1)}, u32[]{:S(2)}, u32[]{:S(2)}) collective-permute-start(bf16[4,16,16,128]{3,2,1,0:T(8,128)(2,1)} %p_ref.1), channel_id=1, source_target_pairs={{0,4},{4,8},{8,12},{12,0},{1,5},{5,9},{9,13},{13,1},{2,6},{6,10},{... | collective-permute-start | bytes 786440 | tf_op jit(solution)/shard_map/ppermute | solution.py:245
  2.1 17.3 %collective-permute-start.1 = (bf16[4,16,16,128]{3,2,1,0:T(8,128)(2,1)}, bf16[4,16,16,128]{3,2,1,0:T(8,128)(2,1)S(1)}, u32[]{:S(2)}, u32[]{:S(2)}) collective-permute-start(bf16[4,16,16,128]{3,2,1,0:T(8,128)(2,1)} %p_ref.1), channel_id=1, source_target_pairs={{4,0},{8,4},{12,8},{0,12},{5,1},{9,5},{13,9},{1,13},{6,2},{10,6},{... | collective-permute-start | bytes 786440 | tf_op jit(solution)/shard_map/ppermute | solution.py:245
  4.1 1.0 %copy-start = (bf16[4,2,32,1024]{3,2,1,0:T(8,128)(2,1)S(1)}, bf16[4,2,32,1024]{3,2,1,0:T(8,128)(2,1)}, u32[]{:S(2)}) copy-start(bf16[4,2,32,1024]{3,2,1,0:T(8,128)(2,1)} %x_ref.1) | copy-start | bytes 1572868
  6.5 15.2 %collective-permute-start.12 = (bf16[128,1024]{1,0:T(8,128)(2,1)S(1)}, bf16[128,1024]{1,0:T(8,128)(2,1)S(1)}, u32[]{:S(2)}, u32[]{:S(2)}) collective-permute-start(bf16[128,1024]{1,0:T(8,128)(2,1)S(1)} %get-tuple-element.24.refs_0_), channel_id=1, source_target_pairs={{0,4},{4,8},{8,12},{12,0},{1,5},{5,9},{9,13},{13,1},{2,6},{6,10},{... | collective-permute-start | bytes 786440 | tf_op jit(solution)/shard_map/ppermute | solution.py:245
  6.5 20.3 %collective-permute-start.13 = (bf16[128,1024]{1,0:T(8,128)(2,1)S(1)}, bf16[128,1024]{1,0:T(8,128)(2,1)S(1)}, u32[]{:S(2)}, u32[]{:S(2)}) collective-permute-start(bf16[128,1024]{1,0:T(8,128)(2,1)S(1)} %get-tuple-element.24.refs_0_), channel_id=1, source_target_pairs={{4,0},{8,4},{12,8},{0,12},{5,1},{9,5},{13,9},{1,13},{6,2},{10,6},{... | collective-permute-start | bytes 786440 | tf_op jit(solution)/shard_map/ppermute | solution.py:245
  9.8 23.2 %collective-permute-start.4 = (bf16[128,512]{1,0:T(8,128)(2,1)S(1)}, bf16[128,512]{1,0:T(8,128)(2,1)S(1)}, u32[]{:S(2)}, u32[]{:S(2)}) collective-permute-start(bf16[128,512]{1,0:T(8,128)(2,1)S(1)} %get-tuple-element.25.refs_2_), channel_id=1, source_target_pairs={{0,4},{4,8},{8,12},{12,0},{1,5},{5,9},{9,13},{13,1},{2,6},{6,10},{... | collective-permute-start | bytes 393224 | tf_op jit(solution)/shard_map/ppermute | solution.py:245
  9.8 2.0 %copy-start.7 = (bf16[4,16,16,128]{3,2,1,0:T(8,128)(2,1)S(1)}, bf16[4,16,16,128]{3,2,1,0:T(8,128)(2,1)}, u32[]{:S(2)}) copy-start(bf16[4,16,16,128]{3,2,1,0:T(8,128)(2,1)} %param.13) | copy-start | bytes 786436
  11.7 1.0 %copy-start.2 = (bf16[4,16,16,128]{3,2,1,0:T(8,128)(2,1)S(1)}, bf16[4,16,16,128]{3,2,1,0:T(8,128)(2,1)}, u32[]{:S(2)}) copy-start(bf16[4,16,16,128]{3,2,1,0:T(8,128)(2,1)} %p_ref.1) | copy-start | bytes 786436
  11.8 0.9 %copy-start.3 = (s32[4,4]{1,0:T(4,128)S(1)}, s32[4,4]{1,0:T(4,128)}, u32[]{:S(2)}) copy-start(s32[4,4]{1,0:T(4,128)} %near_ref.3) | copy-start | bytes 196
  16.2 10.7 %copy-start.1 = (bf16[4,16,2,2,1024]{4,3,2,1,0:T(2,128)(2,1)S(1)}, bf16[4,16,2,2,1024]{4,3,2,1,0:T(2,128)(2,1)}, u32[]{:S(2)}) copy-start(bf16[4,16,2,2,1024]{4,3,2,1,0:T(2,128)(2,1)} %param.16) | copy-start | bytes 1572868
  16.2 17.1 %collective-permute-start.5 = (bf16[128,512]{1,0:T(8,128)(2,1)S(1)}, bf16[128,512]{1,0:T(8,128)(2,1)S(1)}, u32[]{:S(2)}, u32[]{:S(2)}) collective-permute-start(bf16[128,512]{1,0:T(8,128)(2,1)S(1)} %get-tuple-element.25.refs_2_), channel_id=1, source_target_pairs={{4,0},{8,4},{12,8},{0,12},{5,1},{9,5},{13,9},{1,13},{6,2},{10,6},{... | collective-permute-start | bytes 393224 | tf_op jit(solution)/shard_map/ppermute | solution.py:245
  19.4 16.4 %collective-permute-start.2 = (bf16[128,512]{1,0:T(8,128)(2,1)S(1)}, bf16[128,512]{1,0:T(8,128)(2,1)S(1)}, u32[]{:S(2)}, u32[]{:S(2)}) collective-permute-start(bf16[128,512]{1,0:T(8,128)(2,1)S(1)} %get-tuple-element.23.refs_1_), channel_id=1, source_target_pairs={{0,4},{4,8},{8,12},{12,0},{1,5},{5,9},{9,13},{13,1},{2,6},{6,10},{... | collective-permute-start | bytes 393224 | tf_op jit(solution)/shard_map/ppermute | solution.py:245
  21.7 16.4 %collective-permute-start.3 = (bf16[128,512]{1,0:T(8,128)(2,1)S(1)}, bf16[128,512]{1,0:T(8,128)(2,1)S(1)}, u32[]{:S(2)}, u32[]{:S(2)}) collective-permute-start(bf16[128,512]{1,0:T(8,128)(2,1)S(1)} %get-tuple-element.23.refs_1_), channel_id=1, source_target_pairs={{4,0},{8,4},{12,8},{0,12},{5,1},{9,5},{13,9},{1,13},{6,2},{10,6},{... | collective-permute-start | bytes 393224 | tf_op jit(solution)/shard_map/ppermute | solution.py:245
  27.4 13.5 %collective-permute-start.14 = (bf16[4,4,16,128]{3,2,1,0:T(8,128)(2,1)S(1)}, bf16[4,4,16,128]{3,2,1,0:T(8,128)(2,1)S(1)}, u32[]{:S(2)}, u32[]{:S(2)}) collective-permute-start(bf16[4,4,16,128]{3,2,1,0:T(8,128)(2,1)S(1)} %get-tuple-element.38), channel_id=1, source_target_pairs={{0,1},{1,2},{2,3},{3,0},{4,5},{5,6},{6,7},{7,4},{8,9},{9,10},{10,1... | collective-permute-start | bytes 196616 | tf_op jit(solution)/shard_map/ppermute | solution.py:310
  33.0 8.1 %collective-permute-start.15 = (bf16[4,4,16,128]{3,2,1,0:T(8,128)(2,1)S(1)}, bf16[4,4,16,128]{3,2,1,0:T(8,128)(2,1)S(1)}, u32[]{:S(2)}, u32[]{:S(2)}) collective-permute-start(bf16[4,4,16,128]{3,2,1,0:T(8,128)(2,1)S(1)} %get-tuple-element.39), channel_id=1, source_target_pairs={{0,2},{1,3},{2,0},{3,1},{4,6},{5,7},{6,4},{7,5},{8,10},{9,11},{10,... | collective-permute-start | bytes 196616 | tf_op jit(solution)/shard_map/ppermute | solution.py:310
  33.3 9.4 %collective-permute-start.16 = (bf16[4,4,16,128]{3,2,1,0:T(8,128)(2,1)S(1)}, bf16[4,4,16,128]{3,2,1,0:T(8,128)(2,1)S(1)}, u32[]{:S(2)}, u32[]{:S(2)}) collective-permute-start(bf16[4,4,16,128]{3,2,1,0:T(8,128)(2,1)S(1)} %get-tuple-element.40), channel_id=1, source_target_pairs={{0,3},{1,0},{2,1},{3,2},{4,7},{5,4},{6,5},{7,6},{8,11},{9,8},{10,9... | collective-permute-start | bytes 196616 | tf_op jit(solution)/shard_map/ppermute | solution.py:310
  35.8 4.9 %collective-permute-start.11 = (bf16[4,4,8,128]{3,2,1,0:T(8,128)(2,1)S(1)}, bf16[4,4,8,128]{3,2,1,0:T(8,128)(2,1)S(1)}, u32[]{:S(2)}, u32[]{:S(2)}) collective-permute-start(bf16[4,4,8,128]{3,2,1,0:T(8,128)(2,1)S(1)} %get-tuple-element.35), channel_id=1, source_target_pairs={{0,3},{1,0},{2,1},{3,2},{4,7},{5,4},{6,5},{7,6},{8,11},{9,8},{10,9... | collective-permute-start | bytes 98312 | tf_op jit(solution)/shard_map/ppermute | solution.py:310
  38.1 7.2 %collective-permute-start.7 = (bf16[4,4,8,128]{3,2,1,0:T(8,128)(2,1)S(1)}, bf16[4,4,8,128]{3,2,1,0:T(8,128)(2,1)S(1)}, u32[]{:S(2)}, u32[]{:S(2)}) collective-permute-start(bf16[4,4,8,128]{3,2,1,0:T(8,128)(2,1)S(1)} %get-tuple-element.31), channel_id=1, source_target_pairs={{0,1},{1,2},{2,3},{3,0},{4,5},{5,6},{6,7},{7,4},{8,9},{9,10},{10,1... | collective-permute-start | bytes 98312 | tf_op jit(solution)/shard_map/ppermute | solution.py:310
  40.2 3.7 %copy-start.5 = (bf16[256,256]{1,0:T(8,128)(2,1)S(1)}, bf16[256,256]{1,0:T(8,128)(2,1)}, u32[]{:S(2)}) copy-start(bf16[256,256]{1,0:T(8,128)(2,1)} %constant.22.clone.w2_ref) | copy-start | bytes 393220
  40.2 3.7 %copy-start.6 = (f32[2,32,128]{2,1,0:T(8,128)S(1)}, f32[2,32,128]{2,1,0:T(8,128)}, u32[]{:S(2)}) copy-start(f32[2,32,128]{2,1,0:T(8,128)} %constant.21.clone.tw_ref) | copy-start | bytes 98308
  40.7 4.5 %collective-permute-start.9 = (bf16[4,4,8,128]{3,2,1,0:T(8,128)(2,1)S(1)}, bf16[4,4,8,128]{3,2,1,0:T(8,128)(2,1)S(1)}, u32[]{:S(2)}, u32[]{:S(2)}) collective-permute-start(bf16[4,4,8,128]{3,2,1,0:T(8,128)(2,1)S(1)} %get-tuple-element.33), channel_id=1, source_target_pairs={{0,2},{1,3},{2,0},{3,1},{4,6},{5,7},{6,4},{7,5},{8,10},{9,11},{10,... | collective-permute-start | bytes 98312 | tf_op jit(solution)/shard_map/ppermute | solution.py:310
  40.9 4.4 %collective-permute-start.10 = (bf16[4,4,8,128]{3,2,1,0:T(8,128)(2,1)S(1)}, bf16[4,4,8,128]{3,2,1,0:T(8,128)(2,1)S(1)}, u32[]{:S(2)}, u32[]{:S(2)}) collective-permute-start(bf16[4,4,8,128]{3,2,1,0:T(8,128)(2,1)S(1)} %get-tuple-element.34), channel_id=1, source_target_pairs={{0,3},{1,0},{2,1},{3,2},{4,7},{5,4},{6,5},{7,6},{8,11},{9,8},{10,9... | collective-permute-start | bytes 98312 | tf_op jit(solution)/shard_map/ppermute | solution.py:310
  41.2 4.1 %collective-permute-start.6 = (bf16[4,4,8,128]{3,2,1,0:T(8,128)(2,1)S(1)}, bf16[4,4,8,128]{3,2,1,0:T(8,128)(2,1)S(1)}, u32[]{:S(2)}, u32[]{:S(2)}) collective-permute-start(bf16[4,4,8,128]{3,2,1,0:T(8,128)(2,1)S(1)} %get-tuple-element.30), channel_id=1, source_target_pairs={{0,1},{1,2},{2,3},{3,0},{4,5},{5,6},{6,7},{7,4},{8,9},{9,10},{10,1... | collective-permute-start | bytes 98312 | tf_op jit(solution)/shard_map/ppermute | solution.py:310
  42.7 3.3 %collective-permute-start.8 = (bf16[4,4,8,128]{3,2,1,0:T(8,128)(2,1)S(1)}, bf16[4,4,8,128]{3,2,1,0:T(8,128)(2,1)S(1)}, u32[]{:S(2)}, u32[]{:S(2)}) collective-permute-start(bf16[4,4,8,128]{3,2,1,0:T(8,128)(2,1)S(1)} %get-tuple-element.32), channel_id=1, source_target_pairs={{0,2},{1,3},{2,0},{3,1},{4,6},{5,7},{6,4},{7,5},{8,10},{9,11},{10,... | collective-permute-start | bytes 98312 | tf_op jit(solution)/shard_map/ppermute | solution.py:310
  (1 other events, 0.7 us)

commit v2 on v0

--- a/solution.py
+++ b/solution.py
@@ -274,6 +274,11 @@
         )(*ins)
 
     p_before, p_after = both_ways(precoders)
+    base = (lax.axis_index("cell") * cells).astype(jnp.int32)[None]
+    me = lax.axis_index("sc").astype(jnp.int32)[None]
+    w1, twist, w2 = (jnp.asarray(x) for x in tables(length, parts))
+    w1 = lax.dynamic_index_in_dim(w1, me[0], 0, False)
+    plan, base, me, w1 = lax.optimization_barrier((plan, base, me, w1))
     chunks = [(t, 0, blocks) for t in range(times - 1)]
     cut = blocks // 2
     chunks += [(times - 1, 0, cut), (times - 1, cut, blocks - cut)]
@@ -283,8 +288,6 @@
     )
     halos = [both_ways(g) for g in gated]
 
-    base = (lax.axis_index("cell") * cells).astype(jnp.int32)[None]
-    me = lax.axis_index("sc").astype(jnp.int32)[None]
     cross = cross_channel.transpose(3, 2, 0, 1, 4).reshape(subbands, slots * cells * users, ants)
     own = own_channel.transpose(2, 0, 1, 3).reshape(subbands, cells * users, ants)
     noise_tiles = noise.reshape(cells, users, times, 2, blocks, LANES).transpose(0, 1, 2, 4, 3, 5)
@@ -301,8 +304,6 @@
         (neighbours, base, cross, p_before, p_after), 2,
     )
 
-    w1, twist, w2 = (jnp.asarray(x) for x in tables(length, parts))
-    w1 = lax.dynamic_index_in_dim(w1, me[0], 0, False)
     share = users // parts
     full = (cells, share, times, 2 * length // LANES, LANES)
     out, got = None, []
@@ -318,7 +319,9 @@
                 pltpu.VMEM((users, cells, 2 * count, LANES), BF16),
             ],
         )
-        moved = {d: lax.ppermute(sent[d], "sc", [(i, (i ^ d) if ([0, 0, 0])[at] else (i + d) % parts) for i in range(parts)]) for d in ([(3,2,1),(3,2,1),(2,1,3)])[at]}
+        moved = {}
+        for d in range(1, parts):
+            moved[d] = lax.ppermute(sent[d], "sc", [(i, (i + d) % parts) for i in range(parts)])
         got.append([sent[0]] + [moved[d] for d in range(1, parts)])
         if at + 1 < len(chunks) and chunks[at + 1][0] == t:
             continue

time: 48.4 us -> 47.6 us (0.983); the launches traced: 47.4 us -> 47.3 us
  starting transfers between devices: 28.8 us -> 30.3 us
  local copies, waits for them, and re-layouts: 5.35 us -> 4.17 us
    ppermute x8, waiting for transfers between devices: 3.08 us -> 1.73 us  [both_ways(): moved.append(lax.ppermute(x, 'cell', pairs))]
    transpose x1, local copies, waits for them, and re-layouts: 1.95 us -> 0.68 us  [body(): cross_channel.transpose(3, 2, 0, 1, 4)]
    ppermute x9, starting transfers between devices: 15.1 us -> 16.2 us  [body(): lax.ppermute(sent[d], 'sc', [(i, (i + d) % parts) for i in range(parts)])]
    ppermute x9, waiting for transfers between devices: 0.65 us -> 1.55 us  [body(): lax.ppermute(sent[d], 'sc', [(i, (i + d) % parts) for i in range(parts)])]
    unnamed x16 -> x18, local copies, waits for them, and re-layouts: 2.57 us -> 2.66 us
  transfers between devices with their start and end apart: 17 -> 17, of which waited for: 6 -> 4; matrix products, arithmetic and copies ran while one was open for 6% -> 3% of each run, Pallas kernels for 17% -> 17%
where the time goes in v2:
time: 47.6 us; the launch traced here: 47.3 us
  starting transfers between devices  30.3 us (64%)
  Pallas kernels  9.38 us (20%)
  local copies, waits for them, and re-layouts  4.17 us (9%)
  waiting for transfers between devices  3.28 us (7%)
    ppermute x9, starting transfers between devices, body(): lax.ppermute(sent[d], 'sc', [(i, (i + d) % parts) for i in range(parts)])  16.2 us
    ppermute x8, starting transfers between devices, both_ways(): moved.append(lax.ppermute(x, 'cell', pairs))  14.1 us
    pallas_call x6, Pallas kernels, call(): pl.pallas_call(kernel, in_specs=[smem] * scalars + [vmem] * (len(ins) - s...  6.45 us
    pallas_call x2, Pallas kernels, body(): pl.pallas_call(functools.partial(time_kernel, t, halves), in_specs=[vmem]...  2.93 us
    unnamed x18, local copies, waits for them, and re-layouts  2.66 us
    ppermute x8, waiting for transfers between devices, both_ways(): moved.append(lax.ppermute(x, 'cell', pairs))  1.73 us
    ppermute x9, waiting for transfers between devices, body(): lax.ppermute(sent[d], 'sc', [(i, (i + d) % parts) for i in range(parts)])  1.55 us
  transfers between devices with their start and end apart: 17, of which 4 were waited for; matrix products, arithmetic and copies ran while one was open for 3% of the time, Pallas kernels for 17%

profile of v2, /device:TPU:1, one launch (start us, length us, event | category | flops | bytes accessed | tf_op | source)
XLA Modules:
  0.0 47.3 jit_solution(3601638158381598964)
XLA Ops:
  0.0 2.1 %collective-permute-start = (bf16[4,16,16,128]{3,2,1,0:T(8,128)(2,1)}, bf16[4,16,16,128]{3,2,1,0:T(8,128)(2,1)S(1)}, u32[]{:S(2)}, u32[]{:S(2)}) collective-permute-start(bf16[4,16,16,128]{3,2,1,0:T(8,128)(2,1)} %p_ref.1), channel_id=1, source_target_pairs={{0,4},{4,8},{8,12},{12,0},{1,5},{5,9},{9,13},{13,1},{2,6},{6,10},{... | collective-permute-start | bytes 786440 | tf_op jit(solution)/shard_map/ppermute | solution.py:256
  2.1 2.0 %collective-permute-start.1 = (bf16[4,16,16,128]{3,2,1,0:T(8,128)(2,1)}, bf16[4,16,16,128]{3,2,1,0:T(8,128)(2,1)S(1)}, u32[]{:S(2)}, u32[]{:S(2)}) collective-permute-start(bf16[4,16,16,128]{3,2,1,0:T(8,128)(2,1)} %p_ref.1), channel_id=1, source_target_pairs={{4,0},{8,4},{12,8},{0,12},{5,1},{9,5},{13,9},{1,13},{6,2},{10,6},{... | collective-permute-start | bytes 786440 | tf_op jit(solution)/shard_map/ppermute | solution.py:256
  4.1 0.8 %dynamic-slice_bitcast_fusion.w1_ref = bf16[128,64]{1,0:T(8,128)(2,1)S(1)} fusion(bf16[4,128,64]{2,1,0:T(8,128)(2,1)} %constant.20.clone, s32[]{:T(128)S(6)} %select_n.4), kind=kLoop, calls=%fused_computation | loop fusion | bytes 32772 | tf_op jit(solution)/shard_map/jit(dynamic_index_in_dim)/squeeze | solution.py:280
  4.9 0.7 %copy-done.4 = s32[4]{0:T(128)S(1)} copy-done((s32[4]{0:T(128)S(1)}, s32[4]{0:T(128)}, u32[]{:S(2)}) %copy-start.4) | copy-done | bytes 40
  5.6 1.0 %copy-done = bf16[4,2,32,1024]{3,2,1,0:T(8,128)(2,1)S(1)} copy-done((bf16[4,2,32,1024]{3,2,1,0:T(8,128)(2,1)S(1)}, bf16[4,2,32,1024]{3,2,1,0:T(8,128)(2,1)}, u32[]{:S(2)}) %copy-start) | copy-done | bytes 524312
  6.6 0.6 %shard_map.101 = (bf16[128,1024]{1,0:T(8,128)(2,1)S(1)}, bf16[128,512]{1,0:T(8,128)(2,1)S(1)}, bf16[128,512]{1,0:T(8,128)(2,1)S(1)}) custom-call(s32[4]{0:T(128)S(1)} %copy-done.4, bf16[4,2,32,1024]{3,2,1,0:T(8,128)(2,1)S(1)} %copy-done), custom_call_target="tpu_custom_call" | custom-call | flops 1000000000 | bytes 4000000 | tf_op jit(solution)/shard_map/pallas_call | solution.py:266
  7.3 3.3 %collective-permute-start.3 = (bf16[128,512]{1,0:T(8,128)(2,1)S(1)}, bf16[128,512]{1,0:T(8,128)(2,1)S(1)}, u32[]{:S(2)}, u32[]{:S(2)}) collective-permute-start(bf16[128,512]{1,0:T(8,128)(2,1)S(1)} %get-tuple-element.31.refs_1_), channel_id=1, source_target_pairs={{4,0},{8,4},{12,8},{0,12},{5,1},{9,5},{13,9},{1,13},{6,2},{10,6},{... | collective-permute-start | bytes 393224 | tf_op jit(solution)/shard_map/ppermute | solution.py:256
  10.5 0.7 %copy.12 = bf16[16,4,4,16,128]{4,3,2,1,0:T(8,128)(2,1)S(1)} copy(bf16[16,4,4,16,128]{4,0,1,3,2:T(8,128)(2,1)S(1)} %bitcast.24) | data formatting | bytes 2097152 | tf_op jit(solution)/shard_map/transpose | solution.py:291
  11.6 3.3 %collective-permute-start.13 = (bf16[128,1024]{1,0:T(8,128)(2,1)S(1)}, bf16[128,1024]{1,0:T(8,128)(2,1)S(1)}, u32[]{:S(2)}, u32[]{:S(2)}) collective-permute-start(bf16[128,1024]{1,0:T(8,128)(2,1)S(1)} %get-tuple-element.32.refs_0_), channel_id=1, source_target_pairs={{4,0},{8,4},{12,8},{0,12},{5,1},{9,5},{13,9},{1,13},{6,2},{10,6},{... | collective-permute-start | bytes 786440 | tf_op jit(solution)/shard_map/ppermute | solution.py:256
  14.9 0.7 %copy-done.3 = s32[4,4]{1,0:T(4,128)S(1)} copy-done((s32[4,4]{1,0:T(4,128)S(1)}, s32[4,4]{1,0:T(4,128)}, u32[]{:S(2)}) %copy-start.3) | copy-done | bytes 88
  15.6 2.7 %shard_map.102 = (f32[8,128,128]{2,1,0:T(8,128)S(1)}, f32[4,128,128]{2,1,0:T(8,128)S(1)}, f32[4,128,128]{2,1,0:T(8,128)S(1)}) custom-call(s32[4,4]{1,0:T(4,128)S(1)} %copy-done.3, s32[1]{0:T(128)} %bitcast.base_ref, bf16[16,256,128]{2,1,0:T(8,128)(2,1)S(1)} %bitcast.18, bf16[16,64,128]{2,1,0:T(8,128)(2,1)S(1)} %bitcast.20, ...), custom_call_target="tpu_custom_call" | custom-call | flops 1000000000 | bytes 4000000 | tf_op jit(solution)/shard_map/pallas_call | solution.py:266
  18.4 1.9 %shard_map.100.g_ref = bf16[8,256,256]{2,1,0:T(8,128)(2,1)S(1)} custom-call(s32[4,4]{1,0:T(4,128)S(1)} %copy-done.3, s32[1]{0:T(128)} %bitcast.base_ref, bf16[16,256,128]{2,1,0:T(8,128)(2,1)S(1)} %bitcast.19, bf16[4,16,16,128]{3,2,1,0:T(8,128)(2,1)S(1)} %collective-permute-done.a_ref, bf16[4,16,16,128]{3,2,1,0:T(8,128)(2,1)S(1)} %collective-permute-done.1.b_ref), custom_call_target="tpu_custom_call" | custom-call | flops 1000000000 | bytes 4000000 | tf_op jit(solution)/shard_map/pallas_call | solution.py:266
  20.3 3.3 %collective-permute-start.5 = (bf16[128,512]{1,0:T(8,128)(2,1)S(1)}, bf16[128,512]{1,0:T(8,128)(2,1)S(1)}, u32[]{:S(2)}, u32[]{:S(2)}) collective-permute-start(bf16[128,512]{1,0:T(8,128)(2,1)S(1)} %get-tuple-element.33.refs_2_), channel_id=1, source_target_pairs={{4,0},{8,4},{12,8},{0,12},{5,1},{9,5},{13,9},{1,13},{6,2},{10,6},{... | collective-permute-start | bytes 393224 | tf_op jit(solution)/shard_map/ppermute | solution.py:256
  24.0 6.9 %collective-permute-start.6 = (bf16[4,4,8,128]{3,2,1,0:T(8,128)(2,1)S(1)}, bf16[4,4,8,128]{3,2,1,0:T(8,128)(2,1)S(1)}, u32[]{:S(2)}, u32[]{:S(2)}) collective-permute-start(bf16[4,4,8,128]{3,2,1,0:T(8,128)(2,1)S(1)} %get-tuple-element.38), channel_id=1, source_target_pairs={{0,1},{1,2},{2,3},{3,0},{4,5},{5,6},{6,7},{7,4},{8,9},{9,10},{10,1... | collective-permute-start | bytes 98312 | tf_op jit(solution)/shard_map/ppermute | solution.py:324
  30.9 1.6 %collective-permute-done.13.b_ref = bf16[128,1024]{1,0:T(8,128)(2,1)S(1)} collective-permute-done((bf16[128,1024]{1,0:T(8,128)(2,1)S(1)}, bf16[128,1024]{1,0:T(8,128)(2,1)S(1)}, u32[]{:S(2)}, u32[]{:S(2)}) %collective-permute-start.13) | collective-permute-done | bytes 262176 | tf_op jit(solution)/shard_map/ppermute | solution.py:256
  32.5 0.5 %shard_map.105 = (bf16[4,4,16,128]{3,2,1,0:T(8,128)(2,1)S(1)}, bf16[4,4,16,128]{3,2,1,0:T(8,128)(2,1)S(1)}, bf16[4,4,16,128]{3,2,1,0:T(8,128)(2,1)S(1)}, bf16[4,4,16,128]{3,2,1,0:T(8,128)(2,1)S(1)}) custom-call(s32[1]{0:T(128)} %bitcast.1.me_ref, bf16[8,256,256]{2,1,0:T(8,128)(2,1)S(1)} %shard_map.100.g_ref, ...), custom_call_target="tpu_custom_call" | custom-call | flops 1000000000 | bytes 4000000 | tf_op jit(solution)/shard_map/pallas_call | solution.py:266
  33.0 3.9 %collective-permute-start.14 = (bf16[4,4,16,128]{3,2,1,0:T(8,128)(2,1)S(1)}, bf16[4,4,16,128]{3,2,1,0:T(8,128)(2,1)S(1)}, u32[]{:S(2)}, u32[]{:S(2)}) collective-permute-start(bf16[4,4,16,128]{3,2,1,0:T(8,128)(2,1)S(1)} %get-tuple-element.46), channel_id=1, source_target_pairs={{0,1},{1,2},{2,3},{3,0},{4,5},{5,6},{6,7},{7,4},{8,9},{9,10},{10,1... | collective-permute-start | bytes 196616 | tf_op jit(solution)/shard_map/ppermute | solution.py:324
  36.9 1.0 %collective-permute-start.16 = (bf16[4,4,16,128]{3,2,1,0:T(8,128)(2,1)S(1)}, bf16[4,4,16,128]{3,2,1,0:T(8,128)(2,1)S(1)}, u32[]{:S(2)}, u32[]{:S(2)}) collective-permute-start(bf16[4,4,16,128]{3,2,1,0:T(8,128)(2,1)S(1)} %get-tuple-element.48), channel_id=1, source_target_pairs={{0,3},{1,0},{2,1},{3,2},{4,7},{5,4},{6,5},{7,6},{8,11},{9,8},{10,9... | collective-permute-start | bytes 196616 | tf_op jit(solution)/shard_map/ppermute | solution.py:324
  38.4 2.2 %collective-permute-start.7 = (bf16[4,4,8,128]{3,2,1,0:T(8,128)(2,1)S(1)}, bf16[4,4,8,128]{3,2,1,0:T(8,128)(2,1)S(1)}, u32[]{:S(2)}, u32[]{:S(2)}) collective-permute-start(bf16[4,4,8,128]{3,2,1,0:T(8,128)(2,1)S(1)} %get-tuple-element.39), channel_id=1, source_target_pairs={{0,1},{1,2},{2,3},{3,0},{4,5},{5,6},{6,7},{7,4},{8,9},{9,10},{10,1... | collective-permute-start | bytes 98312 | tf_op jit(solution)/shard_map/ppermute | solution.py:324
  40.9 1.2 %collective-permute-start.9 = (bf16[4,4,8,128]{3,2,1,0:T(8,128)(2,1)S(1)}, bf16[4,4,8,128]{3,2,1,0:T(8,128)(2,1)S(1)}, u32[]{:S(2)}, u32[]{:S(2)}) collective-permute-start(bf16[4,4,8,128]{3,2,1,0:T(8,128)(2,1)S(1)} %get-tuple-element.41), channel_id=1, source_target_pairs={{0,2},{1,3},{2,0},{3,1},{4,6},{5,7},{6,4},{7,5},{8,10},{9,11},{10,... | collective-permute-start | bytes 98312 | tf_op jit(solution)/shard_map/ppermute | solution.py:324
  42.1 0.6 %collective-permute-start.11 = (bf16[4,4,8,128]{3,2,1,0:T(8,128)(2,1)S(1)}, bf16[4,4,8,128]{3,2,1,0:T(8,128)(2,1)S(1)}, u32[]{:S(2)}, u32[]{:S(2)}) collective-permute-start(bf16[4,4,8,128]{3,2,1,0:T(8,128)(2,1)S(1)} %get-tuple-element.43), channel_id=1, source_target_pairs={{0,3},{1,0},{2,1},{3,2},{4,7},{5,4},{6,5},{7,6},{8,11},{9,8},{10,9... | collective-permute-start | bytes 98312 | tf_op jit(solution)/shard_map/ppermute | solution.py:324
  42.8 1.5 %time.2.refs_8_ = bf16[4,4,2,64,128]{4,3,2,1,0:T(8,128)(2,1)} custom-call(bf16[128,64]{1,0:T(8,128)(2,1)S(1)} %dynamic-slice_bitcast_fusion.w1_ref, f32[2,32,128]{2,1,0:T(8,128)S(1)} %copy-done.6, bf16[512,256]{1,0:T(8,128)(2,1)S(1)} %copy-done.5, bf16[4,4,16,128]{3,2,1,0:T(8,128)(2,1)S(1)} %get-tuple-element.45.refs_0_, ...), custom_call_target="tpu_custom_call" | custom-call | flops 1000000000 | bytes 2000000 | tf_op jit(solution)/shard_map/time/pallas_call | solution.py:332
  44.3 1.2 %collective-permute-done.10.refs_6_ = bf16[4,4,8,128]{3,2,1,0:T(8,128)(2,1)S(1)} collective-permute-done((bf16[4,4,8,128]{3,2,1,0:T(8,128)(2,1)S(1)}, bf16[4,4,8,128]{3,2,1,0:T(8,128)(2,1)S(1)}, u32[]{:S(2)}, u32[]{:S(2)}) %collective-permute-start.10) | collective-permute-done | bytes 32800 | tf_op jit(solution)/shard_map/ppermute | solution.py:324
  45.8 1.5 %time.3 = bf16[4,4,2,64,128]{4,3,2,1,0:T(8,128)(2,1)} custom-call(bf16[128,64]{1,0:T(8,128)(2,1)S(1)} %dynamic-slice_bitcast_fusion.w1_ref, f32[2,32,128]{2,1,0:T(8,128)S(1)} %copy-done.6, bf16[512,256]{1,0:T(8,128)(2,1)S(1)} %copy-done.5, bf16[4,4,8,128]{3,2,1,0:T(8,128)(2,1)S(1)} %get-tuple-element.35.refs_0_, ...), custom_call_target="tpu_custom_call", output_to_operand_aliasing={{}: (11, {})} | custom-call | flops 1000000000 | bytes 2000000 | tf_op jit(solution)/shard_map/time/pallas_call | solution.py:332
  (39 shorter events, 2.0 us)
Async XLA Ops:
  0.0 11.6 %collective-permute-start = (bf16[4,16,16,128]{3,2,1,0:T(8,128)(2,1)}, bf16[4,16,16,128]{3,2,1,0:T(8,128)(2,1)S(1)}, u32[]{:S(2)}, u32[]{:S(2)}) collective-permute-start(bf16[4,16,16,128]{3,2,1,0:T(8,128)(2,1)} %p_ref.1), channel_id=1, source_target_pairs={{0,4},{4,8},{8,12},{12,0},{1,5},{5,9},{9,13},{13,1},{2,6},{6,10},{... | collective-permute-start | bytes 786440 | tf_op jit(solution)/shard_map/ppermute | solution.py:256
  2.1 16.2 %collective-permute-start.1 = (bf16[4,16,16,128]{3,2,1,0:T(8,128)(2,1)}, bf16[4,16,16,128]{3,2,1,0:T(8,128)(2,1)S(1)}, u32[]{:S(2)}, u32[]{:S(2)}) collective-permute-start(bf16[4,16,16,128]{3,2,1,0:T(8,128)(2,1)} %p_ref.1), channel_id=1, source_target_pairs={{4,0},{8,4},{12,8},{0,12},{5,1},{9,5},{13,9},{1,13},{6,2},{10,6},{... | collective-permute-start | bytes 786440 | tf_op jit(solution)/shard_map/ppermute | solution.py:256
  5.6 1.0 %copy-start = (bf16[4,2,32,1024]{3,2,1,0:T(8,128)(2,1)S(1)}, bf16[4,2,32,1024]{3,2,1,0:T(8,128)(2,1)}, u32[]{:S(2)}) copy-start(bf16[4,2,32,1024]{3,2,1,0:T(8,128)(2,1)} %x_ref.1) | copy-start | bytes 1572868
  6.6 3.9 %copy-start.7 = (bf16[4,16,4,16,128]{4,3,2,1,0:T(8,128)(2,1)S(1)}, bf16[4,16,4,16,128]{4,3,2,1,0:T(8,128)(2,1)}, u32[]{:S(2)}) copy-start(bf16[4,16,4,16,128]{4,3,2,1,0:T(8,128)(2,1)} %param.14) | copy-start | bytes 3145732
  7.2 13.1 %collective-permute-start.2 = (bf16[128,512]{1,0:T(8,128)(2,1)S(1)}, bf16[128,512]{1,0:T(8,128)(2,1)S(1)}, u32[]{:S(2)}, u32[]{:S(2)}) collective-permute-start(bf16[128,512]{1,0:T(8,128)(2,1)S(1)} %get-tuple-element.31.refs_1_), channel_id=1, source_target_pairs={{0,4},{4,8},{8,12},{12,0},{1,5},{5,9},{9,13},{13,1},{2,6},{6,10},{... | collective-permute-start | bytes 393224 | tf_op jit(solution)/shard_map/ppermute | solution.py:256
  7.3 16.3 %collective-permute-start.3 = (bf16[128,512]{1,0:T(8,128)(2,1)S(1)}, bf16[128,512]{1,0:T(8,128)(2,1)S(1)}, u32[]{:S(2)}, u32[]{:S(2)}) collective-permute-start(bf16[128,512]{1,0:T(8,128)(2,1)S(1)} %get-tuple-element.31.refs_1_), channel_id=1, source_target_pairs={{4,0},{8,4},{12,8},{0,12},{5,1},{9,5},{13,9},{1,13},{6,2},{10,6},{... | collective-permute-start | bytes 393224 | tf_op jit(solution)/shard_map/ppermute | solution.py:256
  10.5 20.4 %collective-permute-start.12 = (bf16[128,1024]{1,0:T(8,128)(2,1)S(1)}, bf16[128,1024]{1,0:T(8,128)(2,1)S(1)}, u32[]{:S(2)}, u32[]{:S(2)}) collective-permute-start(bf16[128,1024]{1,0:T(8,128)(2,1)S(1)} %get-tuple-element.32.refs_0_), channel_id=1, source_target_pairs={{0,4},{4,8},{8,12},{12,0},{1,5},{5,9},{9,13},{13,1},{2,6},{6,10},{... | collective-permute-start | bytes 786440 | tf_op jit(solution)/shard_map/ppermute | solution.py:256
  10.5 1.0 %copy-start.8 = (bf16[4,16,16,128]{3,2,1,0:T(8,128)(2,1)S(1)}, bf16[4,16,16,128]{3,2,1,0:T(8,128)(2,1)}, u32[]{:S(2)}) copy-start(bf16[4,16,16,128]{3,2,1,0:T(8,128)(2,1)} %param.13) | copy-start | bytes 786436
  11.5 3.4 %copy-start.2 = (bf16[4,16,16,128]{3,2,1,0:T(8,128)(2,1)S(1)}, bf16[4,16,16,128]{3,2,1,0:T(8,128)(2,1)}, u32[]{:S(2)}) copy-start(bf16[4,16,16,128]{3,2,1,0:T(8,128)(2,1)} %p_ref.1) | copy-start | bytes 786436
  11.6 20.9 %collective-permute-start.13 = (bf16[128,1024]{1,0:T(8,128)(2,1)S(1)}, bf16[128,1024]{1,0:T(8,128)(2,1)S(1)}, u32[]{:S(2)}, u32[]{:S(2)}) collective-permute-start(bf16[128,1024]{1,0:T(8,128)(2,1)S(1)} %get-tuple-element.32.refs_0_), channel_id=1, source_target_pairs={{4,0},{8,4},{12,8},{0,12},{5,1},{9,5},{13,9},{1,13},{6,2},{10,6},{... | collective-permute-start | bytes 786440 | tf_op jit(solution)/shard_map/ppermute | solution.py:256
  18.3 5.3 %copy-start.1 = (bf16[4,16,2,2,1024]{4,3,2,1,0:T(2,128)(2,1)S(1)}, bf16[4,16,2,2,1024]{4,3,2,1,0:T(2,128)(2,1)}, u32[]{:S(2)}) copy-start(bf16[4,16,2,2,1024]{4,3,2,1,0:T(2,128)(2,1)} %param.16) | copy-start | bytes 1572868
  18.3 18.6 %collective-permute-start.4 = (bf16[128,512]{1,0:T(8,128)(2,1)S(1)}, bf16[128,512]{1,0:T(8,128)(2,1)S(1)}, u32[]{:S(2)}, u32[]{:S(2)}) collective-permute-start(bf16[128,512]{1,0:T(8,128)(2,1)S(1)} %get-tuple-element.33.refs_2_), channel_id=1, source_target_pairs={{0,4},{4,8},{8,12},{12,0},{1,5},{5,9},{9,13},{13,1},{2,6},{6,10},{... | collective-permute-start | bytes 393224 | tf_op jit(solution)/shard_map/ppermute | solution.py:256
  20.3 17.8 %collective-permute-start.5 = (bf16[128,512]{1,0:T(8,128)(2,1)S(1)}, bf16[128,512]{1,0:T(8,128)(2,1)S(1)}, u32[]{:S(2)}, u32[]{:S(2)}) collective-permute-start(bf16[128,512]{1,0:T(8,128)(2,1)S(1)} %get-tuple-element.33.refs_2_), channel_id=1, source_target_pairs={{4,0},{8,4},{12,8},{0,12},{5,1},{9,5},{13,9},{1,13},{6,2},{10,6},{... | collective-permute-start | bytes 393224 | tf_op jit(solution)/shard_map/ppermute | solution.py:256
  24.0 16.7 %collective-permute-start.6 = (bf16[4,4,8,128]{3,2,1,0:T(8,128)(2,1)S(1)}, bf16[4,4,8,128]{3,2,1,0:T(8,128)(2,1)S(1)}, u32[]{:S(2)}, u32[]{:S(2)}) collective-permute-start(bf16[4,4,8,128]{3,2,1,0:T(8,128)(2,1)S(1)} %get-tuple-element.38), channel_id=1, source_target_pairs={{0,1},{1,2},{2,3},{3,0},{4,5},{5,6},{6,7},{7,4},{8,9},{9,10},{10,1... | collective-permute-start | bytes 98312 | tf_op jit(solution)/shard_map/ppermute | solution.py:324
  33.0 7.9 %collective-permute-start.14 = (bf16[4,4,16,128]{3,2,1,0:T(8,128)(2,1)S(1)}, bf16[4,4,16,128]{3,2,1,0:T(8,128)(2,1)S(1)}, u32[]{:S(2)}, u32[]{:S(2)}) collective-permute-start(bf16[4,4,16,128]{3,2,1,0:T(8,128)(2,1)S(1)} %get-tuple-element.46), channel_id=1, source_target_pairs={{0,1},{1,2},{2,3},{3,0},{4,5},{5,6},{6,7},{7,4},{8,9},{9,10},{10,1... | collective-permute-start | bytes 196616 | tf_op jit(solution)/shard_map/ppermute | solution.py:324
  36.9 5.2 %collective-permute-start.15 = (bf16[4,4,16,128]{3,2,1,0:T(8,128)(2,1)S(1)}, bf16[4,4,16,128]{3,2,1,0:T(8,128)(2,1)S(1)}, u32[]{:S(2)}, u32[]{:S(2)}) collective-permute-start(bf16[4,4,16,128]{3,2,1,0:T(8,128)(2,1)S(1)} %get-tuple-element.47), channel_id=1, source_target_pairs={{0,2},{1,3},{2,0},{3,1},{4,6},{5,7},{6,4},{7,5},{8,10},{9,11},{10,... | collective-permute-start | bytes 196616 | tf_op jit(solution)/shard_map/ppermute | solution.py:324
  36.9 5.2 %collective-permute-start.16 = (bf16[4,4,16,128]{3,2,1,0:T(8,128)(2,1)S(1)}, bf16[4,4,16,128]{3,2,1,0:T(8,128)(2,1)S(1)}, u32[]{:S(2)}, u32[]{:S(2)}) collective-permute-start(bf16[4,4,16,128]{3,2,1,0:T(8,128)(2,1)S(1)} %get-tuple-element.48), channel_id=1, source_target_pairs={{0,3},{1,0},{2,1},{3,2},{4,7},{5,4},{6,5},{7,6},{8,11},{9,8},{10,9... | collective-permute-start | bytes 196616 | tf_op jit(solution)/shard_map/ppermute | solution.py:324
  38.1 4.7 %copy-start.5 = (bf16[512,256]{1,0:T(8,128)(2,1)S(1)}, bf16[512,256]{1,0:T(8,128)(2,1)}, u32[]{:S(2)}) copy-start(bf16[512,256]{1,0:T(8,128)(2,1)} %constant.22.clone.w2_ref) | copy-start | bytes 786436
  38.1 4.7 %copy-start.6 = (f32[2,32,128]{2,1,0:T(8,128)S(1)}, f32[2,32,128]{2,1,0:T(8,128)}, u32[]{:S(2)}) copy-start(f32[2,32,128]{2,1,0:T(8,128)} %constant.21.clone.tw_ref) | copy-start | bytes 98308
  38.4 5.8 %collective-permute-start.7 = (bf16[4,4,8,128]{3,2,1,0:T(8,128)(2,1)S(1)}, bf16[4,4,8,128]{3,2,1,0:T(8,128)(2,1)S(1)}, u32[]{:S(2)}, u32[]{:S(2)}) collective-permute-start(bf16[4,4,8,128]{3,2,1,0:T(8,128)(2,1)S(1)} %get-tuple-element.39), channel_id=1, source_target_pairs={{0,1},{1,2},{2,3},{3,0},{4,5},{5,6},{6,7},{7,4},{8,9},{9,10},{10,1... | collective-permute-start | bytes 98312 | tf_op jit(solution)/shard_map/ppermute | solution.py:324
  40.6 3.6 %collective-permute-start.8 = (bf16[4,4,8,128]{3,2,1,0:T(8,128)(2,1)S(1)}, bf16[4,4,8,128]{3,2,1,0:T(8,128)(2,1)S(1)}, u32[]{:S(2)}, u32[]{:S(2)}) collective-permute-start(bf16[4,4,8,128]{3,2,1,0:T(8,128)(2,1)S(1)} %get-tuple-element.40), channel_id=1, source_target_pairs={{0,2},{1,3},{2,0},{3,1},{4,6},{5,7},{6,4},{7,5},{8,10},{9,11},{10,... | collective-permute-start | bytes 98312 | tf_op jit(solution)/shard_map/ppermute | solution.py:324
  40.9 3.4 %collective-permute-start.9 = (bf16[4,4,8,128]{3,2,1,0:T(8,128)(2,1)S(1)}, bf16[4,4,8,128]{3,2,1,0:T(8,128)(2,1)S(1)}, u32[]{:S(2)}, u32[]{:S(2)}) collective-permute-start(bf16[4,4,8,128]{3,2,1,0:T(8,128)(2,1)S(1)} %get-tuple-element.41), channel_id=1, source_target_pairs={{0,2},{1,3},{2,0},{3,1},{4,6},{5,7},{6,4},{7,5},{8,10},{9,11},{10,... | collective-permute-start | bytes 98312 | tf_op jit(solution)/shard_map/ppermute | solution.py:324
  42.1 3.3 %collective-permute-start.10 = (bf16[4,4,8,128]{3,2,1,0:T(8,128)(2,1)S(1)}, bf16[4,4,8,128]{3,2,1,0:T(8,128)(2,1)S(1)}, u32[]{:S(2)}, u32[]{:S(2)}) collective-permute-start(bf16[4,4,8,128]{3,2,1,0:T(8,128)(2,1)S(1)} %get-tuple-element.42), channel_id=1, source_target_pairs={{0,3},{1,0},{2,1},{3,2},{4,7},{5,4},{6,5},{7,6},{8,11},{9,8},{10,9... | collective-permute-start | bytes 98312 | tf_op jit(solution)/shard_map/ppermute | solution.py:324
  42.1 3.7 %collective-permute-start.11 = (bf16[4,4,8,128]{3,2,1,0:T(8,128)(2,1)S(1)}, bf16[4,4,8,128]{3,2,1,0:T(8,128)(2,1)S(1)}, u32[]{:S(2)}, u32[]{:S(2)}) collective-permute-start(bf16[4,4,8,128]{3,2,1,0:T(8,128)(2,1)S(1)} %get-tuple-element.43), channel_id=1, source_target_pairs={{0,3},{1,0},{2,1},{3,2},{4,7},{5,4},{6,5},{7,6},{8,11},{9,8},{10,9... | collective-permute-start | bytes 98312 | tf_op jit(solution)/shard_map/ppermute | solution.py:324
  (2 other events, 1.3 us)

commit v3 on v1

--- a/solution.py
+++ b/solution.py
@@ -263,6 +263,11 @@
         )(*ins)
 
     p_before, p_after = both_ways(precoders)
+    base = (lax.axis_index("cell") * cells).astype(jnp.int32)[None]
+    me = lax.axis_index("sc").astype(jnp.int32)[None]
+    w1, twist, w2 = (jnp.asarray(x) for x in tables(length, parts))
+    w1 = lax.dynamic_index_in_dim(w1, me[0], 0, False)
+    plan, base, me, w1 = lax.optimization_barrier((plan, base, me, w1))
     chunks = [(t, 0, blocks) for t in range(times - 1)]
     cut = blocks // 2
     chunks += [(times - 1, 0, cut), (times - 1, cut, blocks - cut)]
@@ -272,8 +277,6 @@
     )
     halos = [both_ways(g) for g in gated]
 
-    base = (lax.axis_index("cell") * cells).astype(jnp.int32)[None]
-    me = lax.axis_index("sc").astype(jnp.int32)[None]
     cross = cross_channel.transpose(3, 2, 0, 1, 4).reshape(subbands, slots * cells * users, ants)
     own = own_channel.transpose(2, 0, 1, 3).reshape(subbands, cells * users, ants)
     noise_tiles = noise.reshape(cells, users, times, 2, blocks, LANES).transpose(0, 1, 2, 4, 3, 5)
@@ -290,8 +293,6 @@
         (neighbours, base, cross, p_before, p_after), 2,
     )
 
-    w1, twist, w2 = (jnp.asarray(x) for x in tables(length, parts))
-    w1 = lax.dynamic_index_in_dim(w1, me[0], 0, False)
     share = users // parts
     full = (cells, share, times, 2 * length // LANES, LANES)
     out, got = None, []
@@ -307,7 +308,9 @@
                 pltpu.VMEM((users, cells, 2 * count, LANES), BF16),
             ],
         )
-        moved = {d: lax.ppermute(sent[d], "sc", [(i, (i ^ d) if ([0, 0, 0])[at] else (i + d) % parts) for i in range(parts)]) for d in ([(3,2,1),(3,2,1),(2,1,3)])[at]}
+        moved = {}
+        for d in range(1, parts):
+            moved[d] = lax.ppermute(sent[d], "sc", [(i, (i + d) % parts) for i in range(parts)])
         got.append([sent[0]] + [moved[d] for d in range(1, parts)])
         if at + 1 < len(chunks) and chunks[at + 1][0] == t:
             continue

time: 48.2 us -> 47.4 us (0.983); the launches traced: 47.2 us -> 47.1 us
  starting transfers between devices: 28.8 us -> 30.3 us
  local copies, waits for them, and re-layouts: 5.31 us -> 4.13 us
  waiting for transfers between devices: 4.01 us -> 3.47 us
    ppermute x8, waiting for transfers between devices: 3.17 us -> 1.73 us  [both_ways(): moved.append(lax.ppermute(x, 'cell', pairs))]
    transpose x1, local copies, waits for them, and re-layouts: 1.95 us -> 0.68 us  [body(): cross_channel.transpose(3, 2, 0, 1, 4)]
    ppermute x9, starting transfers between devices: 15.1 us -> 16.2 us  [body(): lax.ppermute(sent[d], 'sc', [(i, (i + d) % parts) for i in range(parts)])]
    ppermute x9, waiting for transfers between devices: 0.84 us -> 1.74 us  [body(): lax.ppermute(sent[d], 'sc', [(i, (i + d) % parts) for i in range(parts)])]
    unnamed x16 -> x18, local copies, waits for them, and re-layouts: 2.57 us -> 2.66 us
  transfers between devices with their start and end apart: 17 -> 17, of which waited for: 6 -> 4; matrix products, arithmetic and copies ran while one was open for 6% -> 3% of each run, Pallas kernels for 16% -> 16%
where the time goes in v3:
time: 47.4 us; the launch traced here: 47.1 us
  starting transfers between devices  30.3 us (64%)
  Pallas kernels  9.01 us (19%)
  local copies, waits for them, and re-layouts  4.13 us (9%)
  waiting for transfers between devices  3.47 us (7%)
    ppermute x9, starting transfers between devices, body(): lax.ppermute(sent[d], 'sc', [(i, (i + d) % parts) for i in range(parts)])  16.2 us
    ppermute x8, starting transfers between devices, both_ways(): moved.append(lax.ppermute(x, 'cell', pairs))  14.1 us
    pallas_call x6, Pallas kernels, call(): pl.pallas_call(kernel, in_specs=[smem] * scalars + [vmem] * (len(ins) - s...  6.46 us
    unnamed x18, local copies, waits for them, and re-layouts  2.66 us
    pallas_call x2, Pallas kernels, body(): pl.pallas_call(functools.partial(time_kernel, t, halves), in_specs=[vmem]...  2.55 us
    ppermute x9, waiting for transfers between devices, body(): lax.ppermute(sent[d], 'sc', [(i, (i + d) % parts) for i in range(parts)])  1.74 us
    ppermute x8, waiting for transfers between devices, both_ways(): moved.append(lax.ppermute(x, 'cell', pairs))  1.73 us
  transfers between devices with their start and end apart: 17, of which 4 were waited for; matrix products, arithmetic and copies ran while one was open for 3% of the time, Pallas kernels for 16%

profile of v3, /device:TPU:1, one launch (start us, length us, event | category | flops | bytes accessed | tf_op | source)
XLA Modules:
  0.0 47.1 jit_solution(14244683015725496079)
XLA Ops:
  0.0 2.1 %collective-permute-start = (bf16[4,16,16,128]{3,2,1,0:T(8,128)(2,1)}, bf16[4,16,16,128]{3,2,1,0:T(8,128)(2,1)S(1)}, u32[]{:S(2)}, u32[]{:S(2)}) collective-permute-start(bf16[4,16,16,128]{3,2,1,0:T(8,128)(2,1)} %p_ref.1), channel_id=1, source_target_pairs={{0,4},{4,8},{8,12},{12,0},{1,5},{5,9},{9,13},{13,1},{2,6},{6,10},{... | collective-permute-start | bytes 786440 | tf_op jit(solution)/shard_map/ppermute | solution.py:245
  2.1 2.0 %collective-permute-start.1 = (bf16[4,16,16,128]{3,2,1,0:T(8,128)(2,1)}, bf16[4,16,16,128]{3,2,1,0:T(8,128)(2,1)S(1)}, u32[]{:S(2)}, u32[]{:S(2)}) collective-permute-start(bf16[4,16,16,128]{3,2,1,0:T(8,128)(2,1)} %p_ref.1), channel_id=1, source_target_pairs={{4,0},{8,4},{12,8},{0,12},{5,1},{9,5},{13,9},{1,13},{6,2},{10,6},{... | collective-permute-start | bytes 786440 | tf_op jit(solution)/shard_map/ppermute | solution.py:245
  4.1 0.7 %dynamic-slice_bitcast_fusion.w1_ref = bf16[64,64]{1,0:T(8,128)(2,1)S(1)} fusion(bf16[4,64,64]{2,1,0:T(8,128)(2,1)} %constant.20.clone, s32[]{:T(128)S(6)} %select_n.4), kind=kLoop, calls=%fused_computation | loop fusion | bytes 16388 | tf_op jit(solution)/shard_map/jit(dynamic_index_in_dim)/squeeze | solution.py:269
  4.9 0.7 %copy-done.4 = s32[4]{0:T(128)S(1)} copy-done((s32[4]{0:T(128)S(1)}, s32[4]{0:T(128)}, u32[]{:S(2)}) %copy-start.4) | copy-done | bytes 40
  5.5 1.0 %copy-done = bf16[4,2,32,1024]{3,2,1,0:T(8,128)(2,1)S(1)} copy-done((bf16[4,2,32,1024]{3,2,1,0:T(8,128)(2,1)S(1)}, bf16[4,2,32,1024]{3,2,1,0:T(8,128)(2,1)}, u32[]{:S(2)}) %copy-start) | copy-done | bytes 524312
  6.6 0.6 %shard_map.101 = (bf16[128,1024]{1,0:T(8,128)(2,1)S(1)}, bf16[128,512]{1,0:T(8,128)(2,1)S(1)}, bf16[128,512]{1,0:T(8,128)(2,1)S(1)}) custom-call(s32[4]{0:T(128)S(1)} %copy-done.4, bf16[4,2,32,1024]{3,2,1,0:T(8,128)(2,1)S(1)} %copy-done), custom_call_target="tpu_custom_call" | custom-call | flops 1000000000 | bytes 4000000 | tf_op jit(solution)/shard_map/pallas_call | solution.py:255
  7.2 3.3 %collective-permute-start.3 = (bf16[128,512]{1,0:T(8,128)(2,1)S(1)}, bf16[128,512]{1,0:T(8,128)(2,1)S(1)}, u32[]{:S(2)}, u32[]{:S(2)}) collective-permute-start(bf16[128,512]{1,0:T(8,128)(2,1)S(1)} %get-tuple-element.31.refs_1_), channel_id=1, source_target_pairs={{4,0},{8,4},{12,8},{0,12},{5,1},{9,5},{13,9},{1,13},{6,2},{10,6},{... | collective-permute-start | bytes 393224 | tf_op jit(solution)/shard_map/ppermute | solution.py:245
  10.5 0.7 %copy.12 = bf16[16,4,4,16,128]{4,3,2,1,0:T(8,128)(2,1)S(1)} copy(bf16[16,4,4,16,128]{4,0,1,3,2:T(8,128)(2,1)S(1)} %bitcast.24) | data formatting | bytes 2097152 | tf_op jit(solution)/shard_map/transpose | solution.py:280
  11.5 3.3 %collective-permute-start.13 = (bf16[128,1024]{1,0:T(8,128)(2,1)S(1)}, bf16[128,1024]{1,0:T(8,128)(2,1)S(1)}, u32[]{:S(2)}, u32[]{:S(2)}) collective-permute-start(bf16[128,1024]{1,0:T(8,128)(2,1)S(1)} %get-tuple-element.32.refs_0_), channel_id=1, source_target_pairs={{4,0},{8,4},{12,8},{0,12},{5,1},{9,5},{13,9},{1,13},{6,2},{10,6},{... | collective-permute-start | bytes 786440 | tf_op jit(solution)/shard_map/ppermute | solution.py:245
  14.9 0.7 %copy-done.3 = s32[4,4]{1,0:T(4,128)S(1)} copy-done((s32[4,4]{1,0:T(4,128)S(1)}, s32[4,4]{1,0:T(4,128)}, u32[]{:S(2)}) %copy-start.3) | copy-done | bytes 88
  15.5 2.7 %shard_map.102 = (f32[8,128,128]{2,1,0:T(8,128)S(1)}, f32[4,128,128]{2,1,0:T(8,128)S(1)}, f32[4,128,128]{2,1,0:T(8,128)S(1)}) custom-call(s32[4,4]{1,0:T(4,128)S(1)} %copy-done.3, s32[1]{0:T(128)} %bitcast.base_ref, bf16[16,256,128]{2,1,0:T(8,128)(2,1)S(1)} %bitcast.18, bf16[16,64,128]{2,1,0:T(8,128)(2,1)S(1)} %bitcast.20, ...), custom_call_target="tpu_custom_call" | custom-call | flops 1000000000 | bytes 4000000 | tf_op jit(solution)/shard_map/pallas_call | solution.py:255
  18.3 1.9 %shard_map.100.g_ref = bf16[8,256,256]{2,1,0:T(8,128)(2,1)S(1)} custom-call(s32[4,4]{1,0:T(4,128)S(1)} %copy-done.3, s32[1]{0:T(128)} %bitcast.base_ref, bf16[16,256,128]{2,1,0:T(8,128)(2,1)S(1)} %bitcast.19, bf16[4,16,16,128]{3,2,1,0:T(8,128)(2,1)S(1)} %collective-permute-done.a_ref, bf16[4,16,16,128]{3,2,1,0:T(8,128)(2,1)S(1)} %collective-permute-done.1.b_ref), custom_call_target="tpu_custom_call" | custom-call | flops 1000000000 | bytes 4000000 | tf_op jit(solution)/shard_map/pallas_call | solution.py:255
  20.3 3.3 %collective-permute-start.5 = (bf16[128,512]{1,0:T(8,128)(2,1)S(1)}, bf16[128,512]{1,0:T(8,128)(2,1)S(1)}, u32[]{:S(2)}, u32[]{:S(2)}) collective-permute-start(bf16[128,512]{1,0:T(8,128)(2,1)S(1)} %get-tuple-element.33.refs_2_), channel_id=1, source_target_pairs={{4,0},{8,4},{12,8},{0,12},{5,1},{9,5},{13,9},{1,13},{6,2},{10,6},{... | collective-permute-start | bytes 393224 | tf_op jit(solution)/shard_map/ppermute | solution.py:245
  24.0 6.9 %collective-permute-start.6 = (bf16[4,4,8,128]{3,2,1,0:T(8,128)(2,1)S(1)}, bf16[4,4,8,128]{3,2,1,0:T(8,128)(2,1)S(1)}, u32[]{:S(2)}, u32[]{:S(2)}) collective-permute-start(bf16[4,4,8,128]{3,2,1,0:T(8,128)(2,1)S(1)} %get-tuple-element.38), channel_id=1, source_target_pairs={{0,1},{1,2},{2,3},{3,0},{4,5},{5,6},{6,7},{7,4},{8,9},{9,10},{10,1... | collective-permute-start | bytes 98312 | tf_op jit(solution)/shard_map/ppermute | solution.py:313
  30.9 1.6 %collective-permute-done.13.b_ref = bf16[128,1024]{1,0:T(8,128)(2,1)S(1)} collective-permute-done((bf16[128,1024]{1,0:T(8,128)(2,1)S(1)}, bf16[128,1024]{1,0:T(8,128)(2,1)S(1)}, u32[]{:S(2)}, u32[]{:S(2)}) %collective-permute-start.13) | collective-permute-done | bytes 262176 | tf_op jit(solution)/shard_map/ppermute | solution.py:245
  32.5 0.5 %shard_map.105 = (bf16[4,4,16,128]{3,2,1,0:T(8,128)(2,1)S(1)}, bf16[4,4,16,128]{3,2,1,0:T(8,128)(2,1)S(1)}, bf16[4,4,16,128]{3,2,1,0:T(8,128)(2,1)S(1)}, bf16[4,4,16,128]{3,2,1,0:T(8,128)(2,1)S(1)}) custom-call(s32[1]{0:T(128)} %bitcast.1.me_ref, bf16[8,256,256]{2,1,0:T(8,128)(2,1)S(1)} %shard_map.100.g_ref, ...), custom_call_target="tpu_custom_call" | custom-call | flops 1000000000 | bytes 4000000 | tf_op jit(solution)/shard_map/pallas_call | solution.py:255
  33.0 3.9 %collective-permute-start.14 = (bf16[4,4,16,128]{3,2,1,0:T(8,128)(2,1)S(1)}, bf16[4,4,16,128]{3,2,1,0:T(8,128)(2,1)S(1)}, u32[]{:S(2)}, u32[]{:S(2)}) collective-permute-start(bf16[4,4,16,128]{3,2,1,0:T(8,128)(2,1)S(1)} %get-tuple-element.46), channel_id=1, source_target_pairs={{0,1},{1,2},{2,3},{3,0},{4,5},{5,6},{6,7},{7,4},{8,9},{9,10},{10,1... | collective-permute-start | bytes 196616 | tf_op jit(solution)/shard_map/ppermute | solution.py:313
  36.9 1.0 %collective-permute-start.16 = (bf16[4,4,16,128]{3,2,1,0:T(8,128)(2,1)S(1)}, bf16[4,4,16,128]{3,2,1,0:T(8,128)(2,1)S(1)}, u32[]{:S(2)}, u32[]{:S(2)}) collective-permute-start(bf16[4,4,16,128]{3,2,1,0:T(8,128)(2,1)S(1)} %get-tuple-element.48), channel_id=1, source_target_pairs={{0,3},{1,0},{2,1},{3,2},{4,7},{5,4},{6,5},{7,6},{8,11},{9,8},{10,9... | collective-permute-start | bytes 196616 | tf_op jit(solution)/shard_map/ppermute | solution.py:313
  38.4 2.2 %collective-permute-start.7 = (bf16[4,4,8,128]{3,2,1,0:T(8,128)(2,1)S(1)}, bf16[4,4,8,128]{3,2,1,0:T(8,128)(2,1)S(1)}, u32[]{:S(2)}, u32[]{:S(2)}) collective-permute-start(bf16[4,4,8,128]{3,2,1,0:T(8,128)(2,1)S(1)} %get-tuple-element.39), channel_id=1, source_target_pairs={{0,1},{1,2},{2,3},{3,0},{4,5},{5,6},{6,7},{7,4},{8,9},{9,10},{10,1... | collective-permute-start | bytes 98312 | tf_op jit(solution)/shard_map/ppermute | solution.py:313
  40.9 1.2 %collective-permute-start.9 = (bf16[4,4,8,128]{3,2,1,0:T(8,128)(2,1)S(1)}, bf16[4,4,8,128]{3,2,1,0:T(8,128)(2,1)S(1)}, u32[]{:S(2)}, u32[]{:S(2)}) collective-permute-start(bf16[4,4,8,128]{3,2,1,0:T(8,128)(2,1)S(1)} %get-tuple-element.41), channel_id=1, source_target_pairs={{0,2},{1,3},{2,0},{3,1},{4,6},{5,7},{6,4},{7,5},{8,10},{9,11},{10,... | collective-permute-start | bytes 98312 | tf_op jit(solution)/shard_map/ppermute | solution.py:313
  42.1 0.6 %collective-permute-start.11 = (bf16[4,4,8,128]{3,2,1,0:T(8,128)(2,1)S(1)}, bf16[4,4,8,128]{3,2,1,0:T(8,128)(2,1)S(1)}, u32[]{:S(2)}, u32[]{:S(2)}) collective-permute-start(bf16[4,4,8,128]{3,2,1,0:T(8,128)(2,1)S(1)} %get-tuple-element.43), channel_id=1, source_target_pairs={{0,3},{1,0},{2,1},{3,2},{4,7},{5,4},{6,5},{7,6},{8,11},{9,8},{10,9... | collective-permute-start | bytes 98312 | tf_op jit(solution)/shard_map/ppermute | solution.py:313
  42.8 1.3 %time.2.refs_8_ = bf16[4,4,2,64,128]{4,3,2,1,0:T(8,128)(2,1)} custom-call(bf16[64,64]{1,0:T(8,128)(2,1)S(1)} %dynamic-slice_bitcast_fusion.w1_ref, f32[2,32,128]{2,1,0:T(8,128)S(1)} %copy-done.6, bf16[256,256]{1,0:T(8,128)(2,1)S(1)} %copy-done.5, bf16[4,4,16,128]{3,2,1,0:T(8,128)(2,1)S(1)} %get-tuple-element.45.refs_0_, ...), custom_call_target="tpu_custom_call" | custom-call | flops 1000000000 | bytes 2000000 | tf_op jit(solution)/shard_map/time/pallas_call | solution.py:321
  44.1 1.4 %collective-permute-done.10.refs_6_ = bf16[4,4,8,128]{3,2,1,0:T(8,128)(2,1)S(1)} collective-permute-done((bf16[4,4,8,128]{3,2,1,0:T(8,128)(2,1)S(1)}, bf16[4,4,8,128]{3,2,1,0:T(8,128)(2,1)S(1)}, u32[]{:S(2)}, u32[]{:S(2)}) %collective-permute-start.10) | collective-permute-done | bytes 32800 | tf_op jit(solution)/shard_map/ppermute | solution.py:313
  45.8 1.3 %time.3 = bf16[4,4,2,64,128]{4,3,2,1,0:T(8,128)(2,1)} custom-call(bf16[64,64]{1,0:T(8,128)(2,1)S(1)} %dynamic-slice_bitcast_fusion.w1_ref, f32[2,32,128]{2,1,0:T(8,128)S(1)} %copy-done.6, bf16[256,256]{1,0:T(8,128)(2,1)S(1)} %copy-done.5, bf16[4,4,8,128]{3,2,1,0:T(8,128)(2,1)S(1)} %get-tuple-element.35.refs_0_, ...), custom_call_target="tpu_custom_call", output_to_operand_aliasing={{}: (11, {})} | custom-call | flops 1000000000 | bytes 2000000 | tf_op jit(solution)/shard_map/time/pallas_call | solution.py:321
  (39 shorter events, 2.0 us)
Async XLA Ops:
  0.0 11.5 %collective-permute-start = (bf16[4,16,16,128]{3,2,1,0:T(8,128)(2,1)}, bf16[4,16,16,128]{3,2,1,0:T(8,128)(2,1)S(1)}, u32[]{:S(2)}, u32[]{:S(2)}) collective-permute-start(bf16[4,16,16,128]{3,2,1,0:T(8,128)(2,1)} %p_ref.1), channel_id=1, source_target_pairs={{0,4},{4,8},{8,12},{12,0},{1,5},{5,9},{9,13},{13,1},{2,6},{6,10},{... | collective-permute-start | bytes 786440 | tf_op jit(solution)/shard_map/ppermute | solution.py:245
  2.1 16.2 %collective-permute-start.1 = (bf16[4,16,16,128]{3,2,1,0:T(8,128)(2,1)}, bf16[4,16,16,128]{3,2,1,0:T(8,128)(2,1)S(1)}, u32[]{:S(2)}, u32[]{:S(2)}) collective-permute-start(bf16[4,16,16,128]{3,2,1,0:T(8,128)(2,1)} %p_ref.1), channel_id=1, source_target_pairs={{4,0},{8,4},{12,8},{0,12},{5,1},{9,5},{13,9},{1,13},{6,2},{10,6},{... | collective-permute-start | bytes 786440 | tf_op jit(solution)/shard_map/ppermute | solution.py:245
  5.5 1.0 %copy-start = (bf16[4,2,32,1024]{3,2,1,0:T(8,128)(2,1)S(1)}, bf16[4,2,32,1024]{3,2,1,0:T(8,128)(2,1)}, u32[]{:S(2)}) copy-start(bf16[4,2,32,1024]{3,2,1,0:T(8,128)(2,1)} %x_ref.1) | copy-start | bytes 1572868
  6.6 3.9 %copy-start.7 = (bf16[4,16,4,16,128]{4,3,2,1,0:T(8,128)(2,1)S(1)}, bf16[4,16,4,16,128]{4,3,2,1,0:T(8,128)(2,1)}, u32[]{:S(2)}) copy-start(bf16[4,16,4,16,128]{4,3,2,1,0:T(8,128)(2,1)} %param.14) | copy-start | bytes 3145732
  7.2 13.1 %collective-permute-start.2 = (bf16[128,512]{1,0:T(8,128)(2,1)S(1)}, bf16[128,512]{1,0:T(8,128)(2,1)S(1)}, u32[]{:S(2)}, u32[]{:S(2)}) collective-permute-start(bf16[128,512]{1,0:T(8,128)(2,1)S(1)} %get-tuple-element.31.refs_1_), channel_id=1, source_target_pairs={{0,4},{4,8},{8,12},{12,0},{1,5},{5,9},{9,13},{13,1},{2,6},{6,10},{... | collective-permute-start | bytes 393224 | tf_op jit(solution)/shard_map/ppermute | solution.py:245
  7.2 16.3 %collective-permute-start.3 = (bf16[128,512]{1,0:T(8,128)(2,1)S(1)}, bf16[128,512]{1,0:T(8,128)(2,1)S(1)}, u32[]{:S(2)}, u32[]{:S(2)}) collective-permute-start(bf16[128,512]{1,0:T(8,128)(2,1)S(1)} %get-tuple-element.31.refs_1_), channel_id=1, source_target_pairs={{4,0},{8,4},{12,8},{0,12},{5,1},{9,5},{13,9},{1,13},{6,2},{10,6},{... | collective-permute-start | bytes 393224 | tf_op jit(solution)/shard_map/ppermute | solution.py:245
  10.5 20.4 %collective-permute-start.12 = (bf16[128,1024]{1,0:T(8,128)(2,1)S(1)}, bf16[128,1024]{1,0:T(8,128)(2,1)S(1)}, u32[]{:S(2)}, u32[]{:S(2)}) collective-permute-start(bf16[128,1024]{1,0:T(8,128)(2,1)S(1)} %get-tuple-element.32.refs_0_), channel_id=1, source_target_pairs={{0,4},{4,8},{8,12},{12,0},{1,5},{5,9},{9,13},{13,1},{2,6},{6,10},{... | collective-permute-start | bytes 786440 | tf_op jit(solution)/shard_map/ppermute | solution.py:245
  10.5 1.0 %copy-start.8 = (bf16[4,16,16,128]{3,2,1,0:T(8,128)(2,1)S(1)}, bf16[4,16,16,128]{3,2,1,0:T(8,128)(2,1)}, u32[]{:S(2)}) copy-start(bf16[4,16,16,128]{3,2,1,0:T(8,128)(2,1)} %param.13) | copy-start | bytes 786436
  11.5 3.4 %copy-start.2 = (bf16[4,16,16,128]{3,2,1,0:T(8,128)(2,1)S(1)}, bf16[4,16,16,128]{3,2,1,0:T(8,128)(2,1)}, u32[]{:S(2)}) copy-start(bf16[4,16,16,128]{3,2,1,0:T(8,128)(2,1)} %p_ref.1) | copy-start | bytes 786436
  11.5 20.9 %collective-permute-start.13 = (bf16[128,1024]{1,0:T(8,128)(2,1)S(1)}, bf16[128,1024]{1,0:T(8,128)(2,1)S(1)}, u32[]{:S(2)}, u32[]{:S(2)}) collective-permute-start(bf16[128,1024]{1,0:T(8,128)(2,1)S(1)} %get-tuple-element.32.refs_0_), channel_id=1, source_target_pairs={{4,0},{8,4},{12,8},{0,12},{5,1},{9,5},{13,9},{1,13},{6,2},{10,6},{... | collective-permute-start | bytes 786440 | tf_op jit(solution)/shard_map/ppermute | solution.py:245
  18.3 5.3 %copy-start.1 = (bf16[4,16,2,2,1024]{4,3,2,1,0:T(2,128)(2,1)S(1)}, bf16[4,16,2,2,1024]{4,3,2,1,0:T(2,128)(2,1)}, u32[]{:S(2)}) copy-start(bf16[4,16,2,2,1024]{4,3,2,1,0:T(2,128)(2,1)} %param.16) | copy-start | bytes 1572868
  18.3 18.7 %collective-permute-start.4 = (bf16[128,512]{1,0:T(8,128)(2,1)S(1)}, bf16[128,512]{1,0:T(8,128)(2,1)S(1)}, u32[]{:S(2)}, u32[]{:S(2)}) collective-permute-start(bf16[128,512]{1,0:T(8,128)(2,1)S(1)} %get-tuple-element.33.refs_2_), channel_id=1, source_target_pairs={{0,4},{4,8},{8,12},{12,0},{1,5},{5,9},{9,13},{13,1},{2,6},{6,10},{... | collective-permute-start | bytes 393224 | tf_op jit(solution)/shard_map/ppermute | solution.py:245
  20.3 17.8 %collective-permute-start.5 = (bf16[128,512]{1,0:T(8,128)(2,1)S(1)}, bf16[128,512]{1,0:T(8,128)(2,1)S(1)}, u32[]{:S(2)}, u32[]{:S(2)}) collective-permute-start(bf16[128,512]{1,0:T(8,128)(2,1)S(1)} %get-tuple-element.33.refs_2_), channel_id=1, source_target_pairs={{4,0},{8,4},{12,8},{0,12},{5,1},{9,5},{13,9},{1,13},{6,2},{10,6},{... | collective-permute-start | bytes 393224 | tf_op jit(solution)/shard_map/ppermute | solution.py:245
  24.0 16.7 %collective-permute-start.6 = (bf16[4,4,8,128]{3,2,1,0:T(8,128)(2,1)S(1)}, bf16[4,4,8,128]{3,2,1,0:T(8,128)(2,1)S(1)}, u32[]{:S(2)}, u32[]{:S(2)}) collective-permute-start(bf16[4,4,8,128]{3,2,1,0:T(8,128)(2,1)S(1)} %get-tuple-element.38), channel_id=1, source_target_pairs={{0,1},{1,2},{2,3},{3,0},{4,5},{5,6},{6,7},{7,4},{8,9},{9,10},{10,1... | collective-permute-start | bytes 98312 | tf_op jit(solution)/shard_map/ppermute | solution.py:313
  33.0 7.9 %collective-permute-start.14 = (bf16[4,4,16,128]{3,2,1,0:T(8,128)(2,1)S(1)}, bf16[4,4,16,128]{3,2,1,0:T(8,128)(2,1)S(1)}, u32[]{:S(2)}, u32[]{:S(2)}) collective-permute-start(bf16[4,4,16,128]{3,2,1,0:T(8,128)(2,1)S(1)} %get-tuple-element.46), channel_id=1, source_target_pairs={{0,1},{1,2},{2,3},{3,0},{4,5},{5,6},{6,7},{7,4},{8,9},{9,10},{10,1... | collective-permute-start | bytes 196616 | tf_op jit(solution)/shard_map/ppermute | solution.py:313
  36.9 5.2 %collective-permute-start.15 = (bf16[4,4,16,128]{3,2,1,0:T(8,128)(2,1)S(1)}, bf16[4,4,16,128]{3,2,1,0:T(8,128)(2,1)S(1)}, u32[]{:S(2)}, u32[]{:S(2)}) collective-permute-start(bf16[4,4,16,128]{3,2,1,0:T(8,128)(2,1)S(1)} %get-tuple-element.47), channel_id=1, source_target_pairs={{0,2},{1,3},{2,0},{3,1},{4,6},{5,7},{6,4},{7,5},{8,10},{9,11},{10,... | collective-permute-start | bytes 196616 | tf_op jit(solution)/shard_map/ppermute | solution.py:313
  36.9 5.2 %collective-permute-start.16 = (bf16[4,4,16,128]{3,2,1,0:T(8,128)(2,1)S(1)}, bf16[4,4,16,128]{3,2,1,0:T(8,128)(2,1)S(1)}, u32[]{:S(2)}, u32[]{:S(2)}) collective-permute-start(bf16[4,4,16,128]{3,2,1,0:T(8,128)(2,1)S(1)} %get-tuple-element.48), channel_id=1, source_target_pairs={{0,3},{1,0},{2,1},{3,2},{4,7},{5,4},{6,5},{7,6},{8,11},{9,8},{10,9... | collective-permute-start | bytes 196616 | tf_op jit(solution)/shard_map/ppermute | solution.py:313
  38.1 4.7 %copy-start.5 = (bf16[256,256]{1,0:T(8,128)(2,1)S(1)}, bf16[256,256]{1,0:T(8,128)(2,1)}, u32[]{:S(2)}) copy-start(bf16[256,256]{1,0:T(8,128)(2,1)} %constant.22.clone.w2_ref) | copy-start | bytes 393220
  38.1 4.7 %copy-start.6 = (f32[2,32,128]{2,1,0:T(8,128)S(1)}, f32[2,32,128]{2,1,0:T(8,128)}, u32[]{:S(2)}) copy-start(f32[2,32,128]{2,1,0:T(8,128)} %constant.21.clone.tw_ref) | copy-start | bytes 98308
  38.4 5.6 %collective-permute-start.7 = (bf16[4,4,8,128]{3,2,1,0:T(8,128)(2,1)S(1)}, bf16[4,4,8,128]{3,2,1,0:T(8,128)(2,1)S(1)}, u32[]{:S(2)}, u32[]{:S(2)}) collective-permute-start(bf16[4,4,8,128]{3,2,1,0:T(8,128)(2,1)S(1)} %get-tuple-element.39), channel_id=1, source_target_pairs={{0,1},{1,2},{2,3},{3,0},{4,5},{5,6},{6,7},{7,4},{8,9},{9,10},{10,1... | collective-permute-start | bytes 98312 | tf_op jit(solution)/shard_map/ppermute | solution.py:313
  40.6 3.4 %collective-permute-start.8 = (bf16[4,4,8,128]{3,2,1,0:T(8,128)(2,1)S(1)}, bf16[4,4,8,128]{3,2,1,0:T(8,128)(2,1)S(1)}, u32[]{:S(2)}, u32[]{:S(2)}) collective-permute-start(bf16[4,4,8,128]{3,2,1,0:T(8,128)(2,1)S(1)} %get-tuple-element.40), channel_id=1, source_target_pairs={{0,2},{1,3},{2,0},{3,1},{4,6},{5,7},{6,4},{7,5},{8,10},{9,11},{10,... | collective-permute-start | bytes 98312 | tf_op jit(solution)/shard_map/ppermute | solution.py:313
  40.9 3.2 %collective-permute-start.9 = (bf16[4,4,8,128]{3,2,1,0:T(8,128)(2,1)S(1)}, bf16[4,4,8,128]{3,2,1,0:T(8,128)(2,1)S(1)}, u32[]{:S(2)}, u32[]{:S(2)}) collective-permute-start(bf16[4,4,8,128]{3,2,1,0:T(8,128)(2,1)S(1)} %get-tuple-element.41), channel_id=1, source_target_pairs={{0,2},{1,3},{2,0},{3,1},{4,6},{5,7},{6,4},{7,5},{8,10},{9,11},{10,... | collective-permute-start | bytes 98312 | tf_op jit(solution)/shard_map/ppermute | solution.py:313
  42.1 3.3 %collective-permute-start.10 = (bf16[4,4,8,128]{3,2,1,0:T(8,128)(2,1)S(1)}, bf16[4,4,8,128]{3,2,1,0:T(8,128)(2,1)S(1)}, u32[]{:S(2)}, u32[]{:S(2)}) collective-permute-start(bf16[4,4,8,128]{3,2,1,0:T(8,128)(2,1)S(1)} %get-tuple-element.42), channel_id=1, source_target_pairs={{0,3},{1,0},{2,1},{3,2},{4,7},{5,4},{6,5},{7,6},{8,11},{9,8},{10,9... | collective-permute-start | bytes 98312 | tf_op jit(solution)/shard_map/ppermute | solution.py:313
  42.1 3.7 %collective-permute-start.11 = (bf16[4,4,8,128]{3,2,1,0:T(8,128)(2,1)S(1)}, bf16[4,4,8,128]{3,2,1,0:T(8,128)(2,1)S(1)}, u32[]{:S(2)}, u32[]{:S(2)}) collective-permute-start(bf16[4,4,8,128]{3,2,1,0:T(8,128)(2,1)S(1)} %get-tuple-element.43), channel_id=1, source_target_pairs={{0,3},{1,0},{2,1},{3,2},{4,7},{5,4},{6,5},{7,6},{8,11},{9,8},{10,9... | collective-permute-start | bytes 98312 | tf_op jit(solution)/shard_map/ppermute | solution.py:313
  (2 other events, 1.3 us)
